TPU v7x, 32 devices: a whole 2x2x4 slice. The times are simulated.
32 devices in a mesh: dp: 8 (over z, x), fsdp: 4 (over y, core).
Axes of the slice: x: 2, y: 2, z: 4, core: 2. Of those that a mesh axis runs over, the one named last changes fastest.
Arguments:
- frames: bfloat16 [32, 768, 768], P(('dp', 'fsdp')), may hold values from -6 to 6
- lengths: int32 [32], P(('dp', 'fsdp')), may hold values from 1 to 768, 15360 in all
- attn_params: bfloat16 [2363136], P(('dp', 'fsdp')), may hold values from -4 to 4
- ffn_params: bfloat16 [4723968], P(('dp', 'fsdp')), may hold values from -4 to 4
- cotangent: bfloat16 [32, 768, 768], P(('dp', 'fsdp')), may hold values from -6 to 6
Outputs:
- layer_out: bfloat16 [32, 768, 768], P(('dp', 'fsdp'))
- input_grad: bfloat16 [32, 768, 768], P(('dp', 'fsdp'))
- attn_grad: float32 [2363136], P(('dp', 'fsdp'))
- ffn_grad: float32 [4723968], P(('dp', 'fsdp'))
All inputs are finite; a program needn't handle non-finite values. No bound on the sum of `lengths` on one device may be relied on, other than what follows from the above.
Results may differ from a plain program's by a relative error of at most 0.013.
Values may be sent and summed in bfloat16 or wider, within the bound.
A program may use at most 192 MiB of HBM per device.

v0:
```python
from functools import partial

import jax
import jax.numpy as jnp
from jax import lax
from jax.sharding import PartitionSpec as P

D = 768
H = 12
FF = 3072
ATT_LEN = 2363136
FFN_LEN = 4723968


def layer_norm(resid, gain, shift):
    mean = jnp.mean(resid, axis=-1, keepdims=True)
    centered = resid - mean
    var = jnp.mean(centered * centered, axis=-1, keepdims=True)
    return centered * lax.rsqrt(var + 1e-05) * gain + shift


def split_attn(flat):
    square = D * D
    w_qkv = flat[: 3 * square].reshape(D, 3 * D)
    w_out = flat[3 * square : 4 * square].reshape(D, D)
    attn_vec = flat[4 * square : 4 * square + 5 * D].reshape(5, D).astype(jnp.float32)
    return (w_qkv, w_out, attn_vec)


def split_ffn(flat):
    span = D * FF
    w_in = flat[:span].reshape(D, FF)
    w_fc = flat[span : 2 * span].reshape(FF, D)
    b_in = flat[2 * span : 2 * span + FF].astype(jnp.float32)
    ffn_vec = flat[2 * span + FF : 2 * span + FF + 3 * D].reshape(3, D).astype(jnp.float32)
    return (w_in, w_fc, b_in, ffn_vec)


def contract_rows(left, right):
    return lax.dot_general(
        left, right, (((0,), (0,)), ((), ())), preferred_element_type=jnp.float32
    )


def contract_cols(left, right):
    return lax.dot_general(
        left, right, (((1,), (1,)), ((), ())), preferred_element_type=jnp.float32
    )


def masked_scores(query, keys, length):
    scores = contract_cols(query, keys) * 0.125
    live = jnp.arange(keys.shape[0], dtype=jnp.int32) < length
    return jnp.where(live[None, :], scores, -1e30)


def attend(item):
    query, keys, values, length = item
    scores = masked_scores(query, keys, length)
    top = jnp.max(scores, axis=-1, keepdims=True)
    expo = jnp.exp(scores - top)
    total = jnp.sum(expo, axis=-1, keepdims=True)
    probs = (expo / total).astype(jnp.bfloat16)
    mixed = jnp.dot(probs, values, preferred_element_type=jnp.float32)
    return (mixed.astype(jnp.bfloat16), (top + jnp.log(total))[:, 0])


def attend_back(item):
    query, keys, values, grad_mixed, log_total, length = item
    scores = masked_scores(query, keys, length)
    probs = jnp.exp(scores - log_total[:, None])
    grad_p = contract_cols(grad_mixed, values)
    row_dot = jnp.sum(probs * grad_p, axis=-1, keepdims=True)
    grad_s = (probs * (grad_p - row_dot)).astype(jnp.bfloat16)
    grad_q = jnp.dot(grad_s, keys, preferred_element_type=jnp.float32) * 0.125
    grad_k = contract_rows(grad_s, query) * 0.125
    grad_v = contract_rows(probs.astype(jnp.bfloat16), grad_mixed)
    return (grad_q.astype(jnp.bfloat16), grad_k.astype(jnp.bfloat16), grad_v.astype(jnp.bfloat16))


def shards(frames, lengths, attn_params, ffn_params, cotangent):
    utts, span, width = frames.shape
    rows = utts * span
    size = width // H
    devices = lax.axis_size(("dp", "fsdp"))

    def by_heads(part):
        return part.reshape(utts, span, H, size).transpose(0, 2, 1, 3).reshape(utts * H, span, size)

    def from_heads(part):
        return part.reshape(utts, H, span, size).transpose(0, 2, 1, 3).reshape(rows, width)

    attn_flat = lax.all_gather(attn_params, ("dp", "fsdp"), axis=0, tiled=True)
    w_qkv, w_out, attn_vec = split_attn(attn_flat)
    flat_in = frames.reshape(rows, width)
    valid = (
        (jnp.arange(span, dtype=jnp.int32)[None, :] < lengths[:, None])
        .reshape(rows, 1)
        .astype(jnp.float32)
    )
    bias = jnp.concatenate([attn_vec[0], jnp.zeros((width,), jnp.float32), attn_vec[1]])
    qkv_low = (jnp.dot(flat_in, w_qkv, preferred_element_type=jnp.float32) + bias).astype(
        jnp.bfloat16
    )
    query = by_heads(qkv_low[:, :width])
    keys = by_heads(qkv_low[:, width : 2 * width])
    values = by_heads(qkv_low[:, 2 * width :])
    head_len = jnp.repeat(lengths, H)
    mixed_heads, log_total = lax.map(attend, (query, keys, values, head_len))
    mixed_low = from_heads(mixed_heads)
    attn_out = jnp.dot(mixed_low, w_out, preferred_element_type=jnp.float32) + attn_vec[2]
    resid1 = flat_in.astype(jnp.float32) + attn_out
    normed1 = layer_norm(resid1, attn_vec[3], attn_vec[4])
    normed1_low = normed1.astype(jnp.bfloat16)
    ffn_flat = lax.all_gather(ffn_params, ("dp", "fsdp"), axis=0, tiled=True)
    w_in, w_fc, b_in, ffn_vec = split_ffn(ffn_flat)
    pre = jnp.dot(normed1_low, w_in, preferred_element_type=jnp.float32) + b_in
    act_low = jax.nn.gelu(pre, approximate=False).astype(jnp.bfloat16)
    ffn_out = jnp.dot(act_low, w_fc, preferred_element_type=jnp.float32) + ffn_vec[0]
    resid2 = normed1 + ffn_out
    result = layer_norm(resid2, ffn_vec[1], ffn_vec[2]) * valid
    grad_y = cotangent.reshape(rows, width).astype(jnp.float32) * valid
    unused, norm2_back = jax.vjp(layer_norm, resid2, ffn_vec[1], ffn_vec[2])
    grad_r2, grad_g2, grad_b2 = norm2_back(grad_y)
    w_in, w_fc, b_in, ffn_vec = split_ffn(
        lax.all_gather(ffn_params, ("dp", "fsdp"), axis=0, tiled=True)
    )
    grad_f = grad_r2.astype(jnp.bfloat16)
    grad_bfc = jnp.sum(grad_f.astype(jnp.float32), axis=0)
    grad_wfc = contract_rows(act_low, grad_f)
    grad_act = contract_cols(grad_f, w_fc)
    unused, gelu_back = jax.vjp(partial(jax.nn.gelu, approximate=False), pre)
    grad_pre = gelu_back(grad_act)[0].astype(jnp.bfloat16)
    grad_bin = jnp.sum(grad_pre.astype(jnp.float32), axis=0)
    grad_win = contract_rows(normed1_low, grad_pre)
    grad_n1 = grad_r2 + contract_cols(grad_pre, w_in)
    ffn_count = ffn_params.shape[0]
    ffn_terms = jnp.concatenate(
        [
            grad_win.reshape(-1),
            grad_wfc.reshape(-1),
            grad_bin,
            grad_bfc,
            grad_g2,
            grad_b2,
            jnp.zeros((ffn_count * devices - FFN_LEN,), jnp.float32),
        ]
    )
    ffn_grad = lax.psum_scatter(ffn_terms, ("dp", "fsdp"), scatter_dimension=0, tiled=True)
    unused, norm1_back = jax.vjp(layer_norm, resid1, attn_vec[3], attn_vec[4])
    grad_r1, grad_g1, grad_b1 = norm1_back(grad_n1)
    w_qkv, w_out, attn_vec = split_attn(
        lax.all_gather(attn_params, ("dp", "fsdp"), axis=0, tiled=True)
    )
    grad_a = grad_r1.astype(jnp.bfloat16)
    grad_bout = jnp.sum(grad_a.astype(jnp.float32), axis=0)
    grad_wout = contract_rows(mixed_low, grad_a)
    grad_mixed = contract_cols(grad_a, w_out).astype(jnp.bfloat16)
    grad_q, grad_k, grad_v = lax.map(
        attend_back, (query, keys, values, by_heads(grad_mixed), log_total, head_len)
    )
    grad_qkv = jnp.concatenate([from_heads(grad_q), from_heads(grad_k), from_heads(grad_v)], axis=1)
    grad_sums = jnp.sum(grad_qkv.astype(jnp.float32), axis=0)
    grad_wqkv = contract_rows(flat_in, grad_qkv)
    grad_in = grad_r1 + contract_cols(grad_qkv, w_qkv)
    attn_count = attn_params.shape[0]
    attn_terms = jnp.concatenate(
        [
            grad_wqkv.reshape(-1),
            grad_wout.reshape(-1),
            grad_sums[:width],
            grad_sums[2 * width :],
            grad_bout,
            grad_g1,
            grad_b1,
            jnp.zeros((attn_count * devices - ATT_LEN,), jnp.float32),
        ]
    )
    attn_grad = lax.psum_scatter(attn_terms, ("dp", "fsdp"), scatter_dimension=0, tiled=True)
    layer_out = result.reshape(utts, span, width).astype(jnp.bfloat16)
    input_grad = grad_in.reshape(utts, span, width).astype(jnp.bfloat16)
    return (layer_out, input_grad, attn_grad, ffn_grad)


def solution(mesh):
    return jax.shard_map(
        shards,
        mesh=mesh,
        in_specs=(
            P(("dp", "fsdp"), None, None),
            P(("dp", "fsdp")),
            P(("dp", "fsdp")),
            P(("dp", "fsdp")),
            P(("dp", "fsdp"), None, None),
        ),
        out_specs=(
            P(("dp", "fsdp"), None, None),
            P(("dp", "fsdp"), None, None),
            P(("dp", "fsdp")),
            P(("dp", "fsdp")),
        ),
        check_vma=False,
    )
```

profile of v0, /device:TPU:1, one launch (start us, length us, event | category | flops | bytes accessed | tf_op | source)
XLA Modules:
  0.0 1158.6 jit_solution(8447304362163494925)
XLA Ops:
  13.0 4.1 broadcast.239
  17.1 5.8 dynamic-update-slice.1
  26.3 249.4 %all-reduce.11.cloned.1.call-done = (bf16[2363136]{0:T(1024)(128)(2,1)}, bf16[4723968]{0:T(1024)(128)(2,1)}) async-done(((bf16[2363136]{0:T(1024)(128)(2,1)}, bf16[4723968]{0:T(1024)(128)(2,1)}), (bf16[2363136]{0:T(1024)(128)(2,1)}, bf16[4723968]{0:T(1024)(128)(2,1)})) %all-reduce.11.cloned.1.call-update) | async-done | bytes 14174224
  276.4 3.5 slice.132
  285.0 3.9 fusion.82
  289.4 7.6 reshape.258
  297.1 5.4 fusion.60
  307.1 3.7 copy.32
  310.8 3.7 copy.33
  315.7 83.9 %while.26 = (s32[]{:T(128)}, bf16[12,768,64]{1,2,0:T(8,128)(2,1)}, f32[12,768]{1,0:T(8,128)}, s32[12]{0:T(128)S(1)}, bf16[12,768,64]{2,1,0:T(8,128)(2,1)S(1)}, /...) while((s32[]{:T(128)}, bf16[12,768,64]{1,2,0:T(8,128)(2,1)}, ...), condition=%wide.region_3.4_spmd, body=%wide.region_0.3_spmd.sunk | while | flops 158121984 | bytes 7808377 | solution.py:109
  399.6 3.3 slice.118
  402.9 4.5 fusion.86
  407.5 8.2 reshape.267
  415.7 9.2 slice.125
  428.3 30.0 %multiply_convert_fusion.1 = (bf16[768,3072]{1,0:T(8,128)(2,1)S(1)}, f32[768,3072]{1,0:T(8,128)}, f32[768,3072]{1,0:T(8,128)}) fusion(f32[3072]{0:T(1024)S(1)} %copy-done.23, bf16[768,3072]{1,0:T(8,128)(2,1)} %reshape.267, f32[768,768]{0,1:T(8,128)S(1)} %copy-done.3, f32[768]{0:T(1024)S(1)} %copy-done.24, f32[768]{0:T(1024)S(1)} %get-tuple-element.179, ...), kind=kOutput, calls=%fused_computation.64 | convolution fusion | flops 3782541312 | bytes 30695424 | tf_op jit(solution)/shard_map/dot_general | solution.py:117
  458.4 4.7 fusion.87
  465.7 3.3 convert_reduce_fusion.2
  469.0 13.4 %convert_reduce_fusion = (f32[3072]{0:T(1024)}, bf16[768,3072]{1,0:T(8,128)(2,1)}) fusion(f32[768,3072]{1,0:T(8,128)} %get-tuple-element.168, f32[768,3072]{1,0:T(8,128)} %get-tuple-element.191, f32[3072]{0:T(1024)S(1)} %copy-done.23, bf16[768,768]{0,1:T(8,128)(2,1)} %get-tuple-element.160, bf16[3072,768]{1,0:T(8,128)(2,1)S(1)} %bitcast.191), kind=kOutput, calls=%fused_computation.62 | convolution fusion | flops 3663983616 | bytes 29515776 | tf_op jit(solution)/shard_map/dot_general | solution.py:46
  482.4 8.0 multiply_reduce_fusion.1
  501.8 122.4 %while.27 = (s32[]{:T(128)}, bf16[12,768,64]{1,2,0:T(8,128)(2,1)S(1)}, bf16[12,768,64]{1,2,0:T(8,128)(2,1)}, bf16[12,768,64]{1,2,0:T(8,128)(2,1)}, s32[12]{0:T(1...) while((s32[]{:T(128)}, ...), condition=%wide.region_14.15_spmd, body=%wide.region_12.14_spmd.sunk | while | flops 383041536 | bytes 19389548 | solution.py:159
  624.2 8.2 convolution_bitcast_fusion
  634.1 9.0 convolution_bitcast_fusion.1
  643.1 6.5 fusion.89
  649.6 8.0 copy.38
  657.6 7.9 reshape.276
  665.5 5.1 constant_dynamic-update-slice_fusion.2
  677.2 5.9 copy.43
  683.0 3.9 constant_dynamic-update-slice_fusion.3
  686.9 10.8 reshape.279
  700.9 8.3 constant_dynamic-update-slice_fusion.1
  716.7 6.7 fusion.69
  724.8 422.4 %all-reduce.9.cloned.1.call-done = (f32[2363136]{0:T(1024)}, f32[4723968]{0:T(1024)}) async-done(((f32[2363136]{0:T(1024)}, f32[4723968]{0:T(1024)}), (f32[2363136]{0:T(1024)}, f32[4723968]{0:T(1024)})) %all-reduce.9.cloned.1.call-update) | async-done | bytes 28348432
  (362 shorter events, 267.2 us)
Async XLA Ops:
  7.2 268.5 %all-reduce.11.cloned.1.call-start = ((), (), s32[]{:S(2)}) async-start(), calls=%async_computation.1 | async-start | bytes 28352512
  13.0 4.1 copy-start.14
  22.9 1124.3 %all-reduce.9.cloned.1.call-start = ((), (), s32[]{:S(2)}) async-start(), calls=%async_computation | async-start | bytes 56705024
  276.4 8.0 copy-start
  399.6 7.9 copy-start.29
  399.6 3.4 copy-start.26
  424.9 3.4 copy-start.3
  424.9 3.4 copy-start.23
  424.9 3.4 copy-start.24
  424.9 33.4 %slice-start.2 = ((s8[4718592]{0:T(1024)(128)(4,1)}), s8[4194304]{0:T(1024)(128)(4,1)S(1)}, s32[]{:S(2)}) async-start(s8[4718592]{0:T(1024)(128)(4,1)} %bitcast.190), calls=%async_computation.4 | async-start | bytes 8388608
  428.3 62.1 %copy-start.19 = (f32[768]{0:T(1024)}, f32[768]{0:T(1024)S(1)}, u32[]{:S(2)}) copy-start(f32[768]{0:T(1024)S(1)} %get-tuple-element.195) | copy-start | bytes 9220
  428.3 30.0 %slice-start.3 = ((s8[4718592]{0:T(1024)(128)(4,1)}), s8[524288]{0:T(1024)(128)(4,1)S(1)}, s32[]{:S(2)}) async-start(s8[4718592]{0:T(1024)(128)(4,1)} %bitcast.190), calls=%async_computation.5 | async-start | bytes 1048576
  458.3 4.7 copy-start.32
  465.7 16.7 %slice-start = ((s8[4718592]{0:T(1024)(128)(4,1)}), s8[4194304]{0:T(1024)(128)(4,1)S(1)}, s32[]{:S(2)}) async-start(s8[4718592]{0:T(1024)(128)(4,1)} %bitcast.188), calls=%async_computation.2 | async-start | bytes 8388608
  469.0 13.4 %slice-start.1 = ((s8[4718592]{0:T(1024)(128)(4,1)}), s8[524288]{0:T(1024)(128)(4,1)S(1)}, s32[]{:S(2)}) async-start(s8[4718592]{0:T(1024)(128)(4,1)} %bitcast.188), calls=%async_computation.3 | async-start | bytes 1048576
  539.2 3.3 copy-start.31
  559.6 3.3 copy-start.31
  590.1 3.3 copy-start.31
  610.5 3.3 copy-start.31
  624.2 8.2 copy-start.6
  624.2 8.2 copy-start.7
  624.2 8.2 copy-start.8
  632.4 10.7 slice-start.4
  634.1 9.0 copy-start.13
  634.1 9.0 slice-start.5
  686.9 10.8 copy-start.18
  686.9 12.1 %copy-start.28 = (f32[768]{0:T(1024)S(1)}, f32[768]{0:T(1024)}, u32[]{:S(2)}) copy-start(f32[768]{0:T(1024)} %get-tuple-element.113) | copy-start | bytes 9220
  686.9 13.4 %copy-start.27 = (f32[768]{0:T(1024)S(1)}, f32[768]{0:T(1024)}, u32[]{:S(2)}) copy-start(f32[768]{0:T(1024)} %get-tuple-element.119) | copy-start | bytes 9220
  700.9 8.3 copy-start.22
  700.9 8.9 copy-start.21
  700.9 10.2 copy-start.17
  700.9 11.5 copy-start.16
  (20 other events, 50.9 us)
Sparse Core Ops, SparseCore 0:
  23.1 252.5 all-reduce.10
  713.8 433.4 all-reduce.8
where the time goes:
time: 1170 us; the launch traced here: 1160 us
  waiting for transfers between devices  672 us (57%)
  matrix products  239 us (20%)
  local copies, waits for them, and re-layouts  190 us (16%)
  other arithmetic  40.5 us (3%)
  between operations  15.7 us (1%)
    unnamed x4, waiting for transfers between devices  672 us
    dot_general x40, matrix products, contract_cols(): lax.dot_general(left, right, (((1,), (1,)), ((), ())), preferred_element_...  84.8 us
    dot_general x28, matrix products, contract_rows(): lax.dot_general(left, right, (((0,), (0,)), ((), ())), preferred_element_...  65.3 us
    unnamed x98, local copies, waits for them, and re-layouts  61.9 us
    dot_general x1, matrix products, shards(): pre = jnp.dot(normed1_low, w_in, preferred_element_type=jnp.float32) + b_in  30 us
    dot_general x12, matrix products, attend(): mixed = jnp.dot(probs, values, preferred_element_type=jnp.float32)  28.7 us
  transfers between devices with their start and end apart: 2, of which 2 were waited for; matrix products, arithmetic and copies ran while one was open for 1% of the time, Pallas kernels for 0%

commit v1 on v0

v1 whole, which is shorter than its diff:
```python
from functools import partial

import jax
import jax.numpy as jnp
from jax import lax
from jax.experimental import pallas as pl
from jax.experimental.pallas import tpu as pltpu
from jax.sharding import PartitionSpec as P

D = 768
H = 12
FF = 3072
R = 768
PAIRS = 6
ATT_MAT = 4 * D * D
FFN_MAT = 2 * D * FF
ATT_VEC = 5 * D
FFN_VEC = FF + 3 * D
ATT_ROWS = 576
FFN_ROWS = 1152
VEC_ROWS = 80
AXES = ("dp", "fsdp")
bf16 = jnp.bfloat16
f32 = jnp.float32
MESH = pl.DeviceIdType.MESH

B_Q, B_V, B_OUT, G1, B1 = 0, 6, 12, 18, 24
B_IN, B_FC, G2, B2 = 32, 56, 62, 68


def nn(a, b):
    return jnp.dot(a, b, preferred_element_type=f32)


def nt(a, b):
    return lax.dot_general(a, b, (((1,), (1,)), ((), ())), preferred_element_type=f32)


def tn(a, b):
    return lax.dot_general(a, b, (((0,), (0,)), ((), ())), preferred_element_type=f32)


def split3(v):
    hi = v.astype(bf16)
    rest = v - hi.astype(f32)
    mid = rest.astype(bf16)
    return hi, mid, (rest - mid.astype(f32)).astype(bf16)


def place(chunk):
    z, x, y, c = chunk // 8, chunk // 4 % 2, chunk // 2 % 2, chunk % 2
    return z, c, (y * 2 + x if c == 0 else x * 2 + y)


def block(ref, chunk, rows):
    z, c, i = place(chunk)
    return ref[z, c, i, rows, :]


def aligned(start, size):
    return pl.ds(pl.multiple_of(start, size), size)


def w_qkv_pair(attn, i):
    blocks = [block(attn, d, aligned(i * 96, 96)) for d in range(24)]
    return jnp.concatenate(
        [jnp.concatenate([b[32 * p : 32 * p + 32] for b in blocks], axis=0) for p in range(3)], axis=1
    )


def put_w_qkv_pair(attn, i, value):
    for d in range(24):
        z, c, s = place(d)
        for p in range(3):
            attn[z, c, s, pl.ds(pl.multiple_of(i * 96 + 32 * p, 32), 32), :] = value[
                32 * d : 32 * d + 32, 128 * p : 128 * p + 128
            ]


def w_out_cols(attn, j):
    blocks = [block(attn, d, slice(192 * j, 192 * j + 192)) for d in range(24, 32)]
    return jnp.concatenate(
        [jnp.concatenate([b[96 * p : 96 * p + 96] for b in blocks], axis=0) for p in range(2)], axis=1
    )


def w_out_rows(attn, chunks):
    return jnp.concatenate(
        [
            jnp.concatenate([block(attn, d, slice(96 * j, 96 * j + 96)) for j in range(6)], axis=1)
            for d in chunks
        ],
        axis=0,
    )


def w_in_cols(ffn, j, tiles):
    blocks = [block(ffn, d, aligned(j * 48 * tiles, 48 * tiles)) for d in range(16)]
    return jnp.concatenate(
        [jnp.concatenate([b[48 * p : 48 * p + 48] for b in blocks], axis=0) for p in range(tiles)], axis=1
    )


def put_w_in_cols(ffn, j, tiles, value):
    for d in range(16):
        z, c, s = place(d)
        for p in range(tiles):
            ffn[z, c, s, pl.ds(pl.multiple_of(j * 48 * tiles + 48 * p, 48), 48), :] = value[
                48 * d : 48 * d + 48, 128 * p : 128 * p + 128
            ]


def w_fc_cols(ffn, j):
    blocks = [block(ffn, d, aligned(j * 384, 384)) for d in range(16, 32)]
    return jnp.concatenate(
        [jnp.concatenate([b[192 * p : 192 * p + 192] for b in blocks], axis=0) for p in range(2)], axis=1
    )


def chip_slot(m):
    z, x, y = 2 + m // 4, m // 2 % 2, m % 2
    return z, (y * 2 + x, x * 2 + y)


def w_fc_rows(ffn, m):
    z, at = chip_slot(m)
    return jnp.concatenate(
        [
            jnp.concatenate([ffn[z, c, at[c], 192 * j : 192 * j + 192, :] for j in range(6)], axis=1)
            for c in range(2)
        ],
        axis=0,
    )


def put_w_fc_rows(ffn, m, value):
    z, at = chip_slot(m)
    for c in range(2):
        for j in range(6):
            ffn[z, c, at[c], 192 * j : 192 * j + 192, :] = value[192 * c : 192 * c + 192, 128 * j : 128 * j + 128]


def wide(vec, row, n=6):
    return jnp.concatenate([vec[row + j : row + j + 1, :] for j in range(n)], axis=1)


def put_wide(vec, row, value):
    for j in range(value.shape[1] // 128):
        vec[row + j : row + j + 1, :] = value[:, 128 * j : 128 * j + 128]


def lane_ids():
    return lax.broadcasted_iota(jnp.int32, (R, 128), 1)


def attend_pair(qp, kp, vp, dead, lane):
    one, zero = jnp.ones((), bf16), jnp.zeros((), bf16)
    v_one = jnp.concatenate([vp, jnp.ones((R, 128), bf16)], axis=1)
    outs, augmented = [], []
    for h in range(2):
        own = (lane < 64) if h == 0 else (lane >= 64)
        e = 64 if h == 0 else 0
        qh = jnp.where(own, qp, jnp.where(lane == e, one, zero))
        kh = jnp.where(own, kp, jnp.where(lane == e, dead, zero))
        mixed, lses = [], []
        for b in range(3):
            rows = slice(256 * b, 256 * b + 256)
            s = nt(qh[rows], kh)
            top = jnp.max(s, axis=-1, keepdims=True)
            p = jnp.exp(s - top).astype(bf16)
            both = nn(p, v_one)
            total = both[:, 128:]
            mixed.append(both[:, :128] / total)
            lses.append(top + jnp.log(total))
        outs.append(jnp.concatenate(mixed, axis=0))
        hi, mid, low = split3(jnp.concatenate(lses, axis=0))
        for k, part in enumerate((hi, mid, low)):
            qh = jnp.where(lane == e + 1 + k, part, qh)
        augmented.append(qh)
    return jnp.where(lane < 64, outs[0], outs[1]), augmented


def attend_pair_back(q_aug, kp, vp, dop, mixed, dead, lane):
    zero, minus = jnp.zeros((), bf16), -jnp.ones((), bf16)
    weighted = dop.astype(f32) * mixed.astype(f32)
    k_t = kp.T
    dks, dvs, dqs = [], [], []
    for h in range(2):
        own = (lane < 64) if h == 0 else (lane >= 64)
        e = 64 if h == 0 else 0
        dot = jnp.sum(jnp.where(own, weighted, 0.0), axis=-1, keepdims=True)
        do_aug = jnp.where(own, dop, zero)
        for k, part in enumerate(split3(dot)):
            do_aug = jnp.where(lane == e + k, part, do_aug)
        v_aug = jnp.where(own, vp, jnp.where((lane >= e) & (lane < e + 3), minus, zero))
        k_aug = jnp.where(own, kp, jnp.where((lane > e) & (lane < e + 4), minus, jnp.where(lane == e, dead, zero)))
        p = jnp.exp(nt(k_aug, q_aug[h]))
        ds = (p * nt(v_aug, do_aug)).astype(bf16)
        dvs.append(nn(p.astype(bf16), dop))
        dks.append(nn(ds, q_aug[h]))
        dqs.append(nn(k_t, ds))
    row = lax.broadcasted_iota(jnp.int32, (128, R), 0)
    dq = (jnp.where(row < 64, dqs[0], dqs[1]) * 0.125).astype(bf16).T
    dk = jnp.where(lane < 64, dks[0], dks[1]).astype(bf16)
    dv = jnp.where(lane < 64, dvs[0], dvs[1]).astype(bf16)
    return dq, dk, dv


def norm_back(g, xhat, gain, rstd):
    gg = g * gain
    m1 = jnp.mean(gg, axis=-1, keepdims=True)
    m2 = jnp.mean(gg * xhat, axis=-1, keepdims=True)
    return rstd * (gg - m1 - xhat * m2)


def column_sum(v):
    return jnp.sum(v.astype(f32), axis=0, keepdims=True)


ROWS = 128
BLOCKS = R // ROWS


def layer_kernel(gather, refs):
    length = refs["length"][0]
    x, cot = refs["x"], refs["cot"]
    attn, ffn, vec, vg = refs["attn"], refs["ffn"], refs["vec"], refs["vg"]
    qx, kk, vv, mix = refs["qx"], refs["k"], refs["v"], refs["mix"]
    xh1, rs1, n1 = refs["xh1"], refs["rs1"], refs["n1"]
    act, gp, r2, gf, do = refs["act"], refs["gp"], refs["r2"], refs["gf"], refs["do"]
    out, gin = refs["out"], refs["gin"]

    def dead_keys():
        row = lax.broadcasted_iota(jnp.int32, (R, 128), 0)
        return jnp.where(row < length, 0.0, -1e30).astype(bf16)

    gather.start()

    def forward_pair(i, carry):
        gather.before_pair(i)
        lane = lane_ids()
        cols = aligned(i * 128, 128)
        bias = jnp.concatenate(
            [vec[pl.ds(B_Q + i, 1), :], jnp.zeros((1, 128), f32), vec[pl.ds(B_V + i, 1), :]], axis=1
        )
        qkv = (nn(x[...], w_qkv_pair(attn, i)) + bias).astype(bf16)
        qp, kp, vp = qkv[:, :128] * jnp.asarray(0.125, bf16), qkv[:, 128:256], qkv[:, 256:]
        kk[:, cols] = kp
        vv[:, cols] = vp
        mixed, augmented = attend_pair(qp, kp, vp, dead_keys(), lane)
        mix[:, cols] = mixed.astype(bf16)
        for h in range(2):
            qx[:, pl.ds(pl.multiple_of(i * 256 + 128 * h, 128), 128)] = augmented[h]
        return carry

    lax.fori_loop(0, PAIRS, forward_pair, 0)
    gather.step("out")
    for j in range(3):
        cols = slice(256 * j, 256 * j + 256)
        xh1[:, cols] = nn(mix[...], w_out_cols(attn, j)) + wide(vec, B_OUT + 2 * j, 2) + x[:, cols].astype(f32)

    def norm1(b, carry):
        rows = aligned(b * ROWS, ROWS)
        r = xh1[rows, :]
        cen = r - jnp.mean(r, axis=-1, keepdims=True)
        rstd = lax.rsqrt(jnp.mean(cen * cen, axis=-1, keepdims=True) + 1e-05)
        xhat = cen * rstd
        xh1[rows, :] = xhat
        rs1[rows, :] = jnp.broadcast_to(rstd, (ROWS, 128))
        n1[rows, :] = (xhat * wide(vec, G1) + wide(vec, B1)).astype(bf16)
        return carry

    lax.fori_loop(0, BLOCKS, norm1, 0)
    gather.step("norm1")

    def ffn_in(j, carry):
        gather.before_in(j)
        cols = aligned(j * 256, 256)
        bias = jnp.concatenate([vec[pl.ds(B_IN + 2 * j, 1), :], vec[pl.ds(B_IN + 2 * j + 1, 1), :]], axis=1)
        pre = nn(n1[...], w_in_cols(ffn, j, 2)) + bias
        cdf = 0.5 + 0.5 * lax.erf(pre * 0.7071067811865476)
        act[:, cols] = (pre * cdf).astype(bf16)
        gp[:, cols] = (cdf + pre * (jnp.exp(-0.5 * pre * pre) * 0.3989422804014327)).astype(bf16)
        return carry

    lax.fori_loop(0, 12, ffn_in, 0)

    def ffn_out(j, carry):
        gather.before_out(j)
        cols = aligned(j * 256, 256)
        row = lambda base: jnp.concatenate(
            [vec[pl.ds(base + 2 * j, 1), :], vec[pl.ds(base + 2 * j + 1, 1), :]], axis=1
        )
        n1_full = xh1[:, cols] * row(G1) + row(B1)
        r2[:, cols] = nn(act[...], w_fc_cols(ffn, j)) + row(B_FC) + n1_full
        return carry

    lax.fori_loop(0, 3, ffn_out, 0)
    gather.finish()

    def norm2(b, sums):
        rows = aligned(b * ROWS, ROWS)
        r = r2[rows, :]
        cen = r - jnp.mean(r, axis=-1, keepdims=True)
        rstd = lax.rsqrt(jnp.mean(cen * cen, axis=-1, keepdims=True) + 1e-05)
        xhat = cen * rstd
        row = lax.broadcasted_iota(jnp.int32, (ROWS, D), 0) + b * ROWS
        valid = jnp.where(row < length, 1.0, 0.0)
        out[rows, :] = ((xhat * wide(vec, G2) + wide(vec, B2)) * valid).astype(bf16)
        g = cot[rows, :].astype(f32) * valid
        grad = norm_back(g, xhat, wide(vec, G2), rstd)
        r2[rows, :] = grad
        low = grad.astype(bf16)
        gf[rows, :] = low
        return sums[0] + column_sum(g * xhat), sums[1] + column_sum(g), sums[2] + column_sum(low)

    zeros = jnp.zeros((1, D), f32)
    d_g2, d_b2, d_bfc = lax.fori_loop(0, BLOCKS, norm2, (zeros, zeros, zeros))
    put_wide(vg, G2, d_g2)
    put_wide(vg, B2, d_b2)
    put_wide(vg, B_FC, d_bfc)

    def back_fc(m, carry):
        cols = aligned(m * 384, 384)
        grad_act = nt(gf[...], w_fc_rows(ffn, m))
        low = (grad_act * gp[:, cols].astype(f32)).astype(bf16)
        gp[:, cols] = low
        sums = column_sum(low)
        for j in range(3):
            vg[pl.ds(B_IN + 3 * m + j, 1), :] = sums[:, 128 * j : 128 * j + 128]
        put_w_fc_rows(ffn, m, tn(act[:, cols], gf[...]).astype(bf16))
        return carry

    lax.fori_loop(0, 8, back_fc, 0)

    def back_in(j, carry):
        cols = aligned(j * 512, 512)
        g = gp[:, cols]
        r2[...] += nt(g, w_in_cols(ffn, j, 4))
        put_w_in_cols(ffn, j, 4, tn(n1[...], g).astype(bf16))
        return carry

    lax.fori_loop(0, 6, back_in, 0)

    def back_norm1(b, sums):
        rows = aligned(b * ROWS, ROWS)
        g, xhat = r2[rows, :], xh1[rows, :]
        grad = norm_back(g, xhat, wide(vec, G1), rs1[rows, 0:1])
        r2[rows, :] = grad
        low = grad.astype(bf16)
        gf[rows, :] = low
        return sums[0] + column_sum(g * xhat), sums[1] + column_sum(g), sums[2] + column_sum(low)

    d_g1, d_b1, d_bout = lax.fori_loop(0, BLOCKS, back_norm1, (zeros, zeros, zeros))
    put_wide(vg, G1, d_g1)
    put_wide(vg, B1, d_b1)
    put_wide(vg, B_OUT, d_bout)

    for half in range(2):
        do[:, 384 * half : 384 * half + 384] = nt(
            gf[...], w_out_rows(attn, range(24 + 4 * half, 28 + 4 * half))
        ).astype(bf16)
    for half in range(2):
        cols = slice(384 * half, 384 * half + 384)
        grad = tn(mix[:, cols], gf[...]).astype(bf16)
        for d in range(4):
            z, c, s = place(24 + 4 * half + d)
            for j in range(6):
                attn[z, c, s, 96 * j : 96 * j + 96, :] = grad[96 * d : 96 * d + 96, 128 * j : 128 * j + 128]

    def backward_pair(i, carry):
        lane = lane_ids()
        cols = aligned(i * 128, 128)
        q_aug = [qx[:, pl.ds(pl.multiple_of(i * 256 + 128 * h, 128), 128)] for h in range(2)]
        dq, dk, dv = attend_pair_back(q_aug, kk[:, cols], vv[:, cols], do[:, cols], mix[:, cols], dead_keys(), lane)
        vg[pl.ds(B_Q + i, 1), :] = column_sum(dq)
        vg[pl.ds(B_V + i, 1), :] = column_sum(dv)
        grad = jnp.concatenate([dq, dk, dv], axis=1)
        r2[...] += nt(grad, w_qkv_pair(attn, i))
        put_w_qkv_pair(attn, i, tn(x[...], grad).astype(bf16))
        return carry

    lax.fori_loop(0, PAIRS, backward_pair, 0)
    gin[...] = r2[...].astype(bf16)


class Loaded:
    def __init__(self, refs):
        self.refs = refs

    def start(self):
        r = self.refs
        copies = [
            pltpu.make_async_copy(r["attn_in"], r["attn"], r["sems"].at[0]),
            pltpu.make_async_copy(r["ffn_in"], r["ffn"], r["sems"].at[1]),
        ]
        for c in copies:
            c.start()
        r["vec"][...] = r["vec_in"][...].astype(f32)
        for c in copies:
            c.wait()

    def before_pair(self, i):
        pass

    before_in = before_out = step = before_pair

    def finish(self):
        pass


def position():
    dp, fs = lax.axis_index("dp"), lax.axis_index("fsdp")
    return lax.div(dp, 2), lax.rem(dp, 2), lax.div(fs, 2), lax.rem(fs, 2)


def device(z, x, y, c):
    return (z * 2 + x, y * 2 + c)


def remote(src, dst, send, recv, target):
    return pltpu.make_async_remote_copy(
        src_ref=src, dst_ref=dst, send_sem=send, recv_sem=recv, device_id=target, device_id_type=MESH
    )


GROUPS = 10


class Gather:
    def __init__(self, refs):
        self.refs = refs
        self.z, self.x, self.y, self.c = z, x, y, c = position()
        first = c == 0
        a, b = jnp.where(first, x, y), jnp.where(first, y, x)
        self.slot, self.pair = b * 2 + a, b * 2
        self.other_slot, self.other_pair = b * 2 + 1 - a, (1 - b) * 2
        self.dev_a = device(z, jnp.where(first, 1 - x, x), jnp.where(first, y, 1 - y), c)
        self.dev_b = device(z, jnp.where(first, x, 1 - x), jnp.where(first, 1 - y, y), c)
        self.dev_c = device(z, x, y, 1 - c)
        self.zs = [lax.rem(z + k, 4) for k in (1, 2, 3)]
        self.dev_z = [device(t, x, y, c) for t in self.zs]

    def barrier(self):
        bar = pltpu.get_barrier_semaphore()
        targets = [self.dev_a, self.dev_b, self.dev_c] + self.dev_z
        for t in targets:
            pl.semaphore_signal(bar, inc=1, device_id=t, device_id_type=MESH)
        pl.semaphore_wait(bar, len(targets))

    def part(self, g):
        if isinstance(g, int) and g >= PAIRS:
            n = g - PAIRS
            return self.refs["ffn"], (slice(0, 2) if n < 2 else slice(2, 4)), slice(576 * (n % 2), 576 * (n % 2) + 576)
        return self.refs["attn"], slice(0, 4), aligned(g * 96, 96)

    def send_z(self, g):
        buf, zz, rows = self.part(g)
        own = self.refs["own_a"] if buf is self.refs["attn"] else self.refs["own_f"]
        r = self.refs

        def go():
            dst = buf.at[self.z, self.c, self.slot, rows]
            pltpu.make_async_copy(own.at[rows], dst, r["own_sem"].at[g]).start()
            for k in range(3):
                remote(own.at[rows], dst, r["zs"].at[g, k], r["zr"].at[g, k], self.dev_z[k]).start()

        self.if_in(zz, go)

    def if_in(self, zz, fn):
        if zz == slice(0, 4):
            fn()
        else:
            pl.when((self.z >= zz.start) & (self.z < zz.stop))(fn)

    def relay_a(self, g):
        buf, zz, rows = self.part(g)
        r = self.refs
        one = buf.at[self.z, self.c, self.slot, rows]
        own = self.refs["own_a"] if buf is self.refs["attn"] else self.refs["own_f"]
        self.if_in(zz, lambda: pltpu.make_async_copy(own.at[rows], one, r["own_sem"].at[g]).wait())
        for k in range(3):
            source = lax.rem(self.z + 3 - k, 4)

            def got(k=k, source=source):
                dst = buf.at[source, self.c, self.slot, rows]
                remote(dst, dst, r["zs"].at[g, k], r["zr"].at[g, k], self.dev_z[k]).wait_recv()

            if zz == slice(0, 4):
                got()
            else:
                pl.when((source >= zz.start) & (source < zz.stop))(got)
        mine = buf.at[zz, self.c, self.slot, rows]
        remote(mine, mine, r["as"].at[g], r["ar"].at[g], self.dev_a).start()

    def relay_b(self, g):
        buf, zz, rows = self.part(g)
        r = self.refs
        got = buf.at[zz, self.c, self.other_slot, rows]
        remote(got, got, r["as"].at[g], r["ar"].at[g], self.dev_a).wait_recv()
        mine = buf.at[zz, self.c, pl.ds(self.pair, 2), rows]
        remote(mine, mine, r["bs"].at[g], r["br"].at[g], self.dev_b).start()

    def relay_c(self, g):
        buf, zz, rows = self.part(g)
        r = self.refs
        got = buf.at[zz, self.c, pl.ds(self.other_pair, 2), rows]
        remote(got, got, r["bs"].at[g], r["br"].at[g], self.dev_b).wait_recv()
        mine = buf.at[zz, self.c, :, rows]
        remote(mine, mine, r["cs"].at[g], r["cr"].at[g], self.dev_c).start()

    def ready(self, g):
        buf, zz, rows = self.part(g)
        r = self.refs
        got = buf.at[zz, 1 - self.c, :, rows]
        remote(got, got, r["cs"].at[g], r["cr"].at[g], self.dev_c).wait_recv()

    def vectors(self, stage):
        r = self.refs
        buf, own = r["vec_all"], r["own_v"]
        one = buf.at[self.c, self.slot]
        if stage == 0:

            @pl.when(self.z == 3)
            def _():
                pltpu.make_async_copy(own, one, r["vsem"].at[0]).start()
                for k in range(3):
                    remote(own, one, r["vsem"].at[4 + k], r["vsem"].at[1], self.dev_z[k]).start()

        elif stage == 1:

            @pl.when(self.z == 3)
            def _():
                pltpu.make_async_copy(own, one, r["vsem"].at[0]).wait()
                for k in range(3):
                    remote(own, one, r["vsem"].at[4 + k], r["vsem"].at[1], self.dev_z[k]).wait_send()

            @pl.when(self.z != 3)
            def _():
                remote(one, one, r["vsem"].at[4], r["vsem"].at[1], self.dev_z[0]).wait_recv()

            remote(one, one, r["vsem"].at[7], r["vsem"].at[2], self.dev_a).start()
        elif stage == 2:
            got = buf.at[self.c, self.other_slot]
            remote(got, got, r["vsem"].at[7], r["vsem"].at[2], self.dev_a).wait()
            mine = buf.at[self.c, pl.ds(self.pair, 2)]
            remote(mine, mine, r["vsem"].at[8], r["vsem"].at[3], self.dev_b).start()
        elif stage == 3:
            got = buf.at[self.c, pl.ds(self.other_pair, 2)]
            remote(got, got, r["vsem"].at[8], r["vsem"].at[3], self.dev_b).wait()
            mine = buf.at[self.c]
            remote(mine, mine, r["vsem"].at[9], r["vsem"].at[10], self.dev_c).start()
        else:
            got = buf.at[1 - self.c]
            remote(got, got, r["vsem"].at[9], r["vsem"].at[10], self.dev_c).wait()
            r["vec"][...] = buf[1, 3].astype(f32)

    def start(self):
        self.barrier()
        self.vectors(0)
        for g in range(GROUPS):
            self.send_z(g)
        self.vectors(1)
        self.relay_a(0)
        self.vectors(2)
        self.relay_b(0)
        self.relay_a(1)
        self.vectors(3)
        self.relay_c(0)
        self.relay_b(1)
        self.relay_a(2)
        self.vectors(4)

    def before_pair(self, i):
        @pl.when(i + 3 < PAIRS)
        def _():
            self.relay_a(i + 3)

        @pl.when(i + 2 < PAIRS)
        def _():
            self.relay_b(i + 2)

        @pl.when(i + 1 < PAIRS)
        def _():
            self.relay_c(i + 1)

        @pl.when(i == 3)
        def _():
            self.relay_a(6)

        @pl.when(i == 4)
        def _():
            self.relay_b(6)

        @pl.when(i == 5)
        def _():
            self.relay_a(7)

        self.ready(i)

    def step(self, name):
        if name == "out":
            self.relay_c(6)
            self.relay_b(7)
            self.relay_a(8)
        elif name == "norm1":
            self.ready(6)

    def before_in(self, j):
        @pl.when(j == 2)
        def _():
            self.relay_c(7)
            self.relay_b(8)
            self.relay_a(9)

        @pl.when(j == 6)
        def _():
            self.ready(7)

        @pl.when(j == 9)
        def _():
            self.relay_c(8)
            self.relay_b(9)

    def before_out(self, j):
        @pl.when(j == 0)
        def _():
            self.ready(8)
            self.relay_c(9)
            self.ready(9)

    def finish(self):
        r = self.refs
        for g in range(GROUPS):
            buf, zz, rows = self.part(g)
            own = r["own_a"] if buf is r["attn"] else r["own_f"]

            def sent(g=g, own=own, rows=rows, buf=buf):
                dst = buf.at[self.z, self.c, self.slot, rows]
                for k in range(3):
                    remote(own.at[rows], dst, r["zs"].at[g, k], r["zr"].at[g, k], self.dev_z[k]).wait_send()

            self.if_in(zz, sent)
            for refs, s, v, t in (
                (buf.at[zz, self.c, self.slot, rows], "as", "ar", self.dev_a),
                (buf.at[zz, self.c, pl.ds(self.pair, 2), rows], "bs", "br", self.dev_b),
                (buf.at[zz, self.c, :, rows], "cs", "cr", self.dev_c),
            ):
                remote(refs, refs, r[s].at[g], r[v].at[g], t).wait_send()


SCRATCH = dict(
    attn=((4, 2, 4, ATT_ROWS, 128), bf16),
    ffn=((4, 2, 4, FFN_ROWS, 128), bf16),
    vec=((VEC_ROWS, 128), f32),
    qx=((R, 1536), bf16),
    k=((R, D), bf16),
    v=((R, D), bf16),
    mix=((R, D), bf16),
    xh1=((R, D), f32),
    rs1=((R, 128), f32),
    n1=((R, D), bf16),
    act=((R, FF), bf16),
    gp=((R, FF), bf16),
    r2=((R, D), f32),
    gf=((R, D), bf16),
    do=((R, D), bf16),
)


def run_layer(linked, length, x, cot, attn_in, ffn_in, vec_in):
    dma = pltpu.SemaphoreType.DMA
    vmem, anywhere = pl.BlockSpec(memory_space=pltpu.VMEM), pl.BlockSpec(memory_space=pl.ANY)
    names = ["length", "x", "cot"] + (["own_a", "own_f", "own_v"] if linked else ["attn_in", "ffn_in", "vec_in"])
    names += ["out", "gin", "attn_g", "ffn_g", "vg"]
    scratch = [pltpu.VMEM(*s) for s in SCRATCH.values()]
    names += list(SCRATCH)
    if linked:
        sems = dict(
            vec_all=pltpu.VMEM((2, 4, VEC_ROWS, 128), bf16),
            own_sem=dma((GROUPS,)),
            zs=dma((GROUPS, 3)),
            zr=dma((GROUPS, 3)),
            vsem=dma((11,)),
            **{k: dma((GROUPS,)) for k in ("as", "ar", "bs", "br", "cs", "cr")},
        )
    else:
        sems = {}
    sems["sems"] = dma((2,))
    scratch += list(sems.values())
    names += list(sems)

    def body(*args):
        refs = dict(zip(names, args, strict=True))
        refs["vg"][...] = jnp.zeros((VEC_ROWS, 128), f32)
        layer_kernel((Gather if linked else Loaded)(refs), refs)
        copies = [
            pltpu.make_async_copy(refs["attn"], refs["attn_g"], refs["sems"].at[0]),
            pltpu.make_async_copy(refs["ffn"], refs["ffn_g"], refs["sems"].at[1]),
        ]
        for c in copies:
            c.start()
        for c in copies:
            c.wait()

    big = anywhere if not linked else vmem
    return pl.pallas_call(
        body,
        out_shape=(
            jax.ShapeDtypeStruct((R, D), bf16),
            jax.ShapeDtypeStruct((R, D), bf16),
            jax.ShapeDtypeStruct(SCRATCH["attn"][0], bf16),
            jax.ShapeDtypeStruct(SCRATCH["ffn"][0], bf16),
            jax.ShapeDtypeStruct((VEC_ROWS, 128), f32),
        ),
        in_specs=[pl.BlockSpec(memory_space=pltpu.SMEM), vmem, vmem, big, big, vmem],
        out_specs=(vmem, vmem, anywhere, anywhere, vmem),
        scratch_shapes=scratch,
        compiler_params=pltpu.CompilerParams(
            vmem_limit_bytes=64 * 1024 * 1024 - 65536,
            has_side_effects=True,
            **(dict(collective_id=0) if linked else {}),
        ),
    )(length, x, cot, attn_in, ffn_in, vec_in)


def qkv_chunk(flat):
    return flat.reshape(-1, 32, 3, 6, 128).transpose(0, 3, 2, 1, 4).reshape(-1, ATT_ROWS, 128)


def qkv_flat(chunk):
    return chunk.reshape(-1, 6, 3, 32, 128).transpose(0, 3, 2, 1, 4).reshape(-1)


def tiled_chunk(flat, rows, tiles):
    return flat.reshape(-1, rows, tiles, 128).transpose(0, 2, 1, 3).reshape(-1, rows * tiles, 128)


def tiled_flat(chunk, rows, tiles):
    return chunk.reshape(-1, tiles, rows, 128).transpose(0, 2, 1, 3).reshape(-1)


def pack_vectors(attn_vec, ffn_vec):
    return jnp.concatenate(
        [
            attn_vec.reshape(30, 128),
            jnp.zeros((2, 128), attn_vec.dtype),
            ffn_vec.reshape(42, 128),
            jnp.zeros((6, 128), attn_vec.dtype),
        ]
    )


def shards_linked(frames, lengths, attn_params, ffn_params, cotangent):
    me = lax.axis_index("dp") * 4 + lax.axis_index("fsdp")
    z = me // 8
    tails = jnp.concatenate([attn_params[-ATT_VEC:], ffn_params[-FFN_VEC:]])
    before = lax.ppermute(tails, AXES, [(i, i + 1) for i in range(31)])
    a = lax.dynamic_slice(
        jnp.concatenate([before[:ATT_VEC], attn_params]), (ATT_VEC - 120 * me,), (ATT_ROWS * 128,)
    )
    f = lax.dynamic_slice(
        jnp.concatenate([before[ATT_VEC:], ffn_params]), (FFN_VEC - 168 * me,), (FFN_ROWS * 128,)
    )
    own_a = jnp.where(z == 3, tiled_chunk(a, 96, 6)[0], qkv_chunk(a)[0])
    own_f = jnp.where(z >= 2, tiled_chunk(f, 192, 6)[0], tiled_chunk(f, 48, 24)[0])
    own_v = pack_vectors(tails[:ATT_VEC], tails[ATT_VEC:])
    out, gin, attn_g, ffn_g, vg = run_layer(True, lengths, frames[0], cotangent[0], own_a, own_f, own_v)

    def scatter(g):
        p0 = g[:, 0].reshape(4, 2, 2, -1, 128).transpose(0, 2, 1, 3, 4)
        p1 = g[:, 1].reshape(4, 2, 2, -1, 128)
        chunks = jnp.stack([p0, p1], axis=3).reshape(32, -1, 128)
        return lax.psum_scatter(chunks.astype(f32), AXES, scatter_dimension=0, tiled=True)[0]

    ga, gfn, vsum = scatter(attn_g), scatter(ffn_g), lax.psum(vg, AXES)
    a = jnp.where(z == 3, tiled_flat(ga, 96, 6), qkv_flat(ga))
    f = jnp.where(z >= 2, tiled_flat(gfn, 192, 6), tiled_flat(gfn, 48, 24))
    heads = jnp.concatenate([a[:ATT_VEC], f[:FFN_VEC]])
    vecs = jnp.concatenate([vsum[:30].reshape(-1), vsum[32:74].reshape(-1)])
    after = jnp.where(me == 31, vecs, lax.ppermute(heads, AXES, [(i + 1, i) for i in range(31)]))
    attn_grad = lax.dynamic_slice(jnp.concatenate([a, after[:ATT_VEC]]), (120 * me,), attn_params.shape)
    ffn_grad = lax.dynamic_slice(jnp.concatenate([f, after[ATT_VEC:]]), (168 * me,), ffn_params.shape)
    return out[None], gin[None], attn_grad, ffn_grad


def in_places(chunks):
    g = chunks.reshape(4, 2, 2, 2, -1, 128)
    p0 = g[:, :, :, 0].transpose(0, 2, 1, 3, 4).reshape(4, 4, -1, 128)
    p1 = g[:, :, :, 1].reshape(4, 4, -1, 128)
    return jnp.stack([p0, p1], axis=1)


def from_places(g):
    p0 = g[:, 0].reshape(4, 2, 2, -1, 128).transpose(0, 2, 1, 3, 4)
    p1 = g[:, 1].reshape(4, 2, 2, -1, 128)
    return jnp.stack([p0, p1], axis=3).reshape(32, -1, 128)


def shards_any(frames, lengths, attn_params, ffn_params, cotangent):
    devices = lax.axis_size(AXES)
    attn_flat = lax.all_gather(attn_params, AXES, axis=0, tiled=True)
    ffn_flat = lax.all_gather(ffn_params, AXES, axis=0, tiled=True)
    cut_a, cut_f = 3 * D * D, D * FF
    attn_in = in_places(
        jnp.concatenate([qkv_chunk(attn_flat[:cut_a]), tiled_chunk(attn_flat[cut_a:ATT_MAT], 96, 6)])
    )
    ffn_in = in_places(
        jnp.concatenate([tiled_chunk(ffn_flat[:cut_f], 48, 24), tiled_chunk(ffn_flat[cut_f:FFN_MAT], 192, 6)])
    )
    vec_in = pack_vectors(attn_flat[ATT_MAT : ATT_MAT + ATT_VEC], ffn_flat[FFN_MAT : FFN_MAT + FFN_VEC])
    outs, gins, sums = [], [], None
    for u in range(frames.shape[0]):
        out, gin, *grads = run_layer(False, lengths[u : u + 1], frames[u], cotangent[u], attn_in, ffn_in, vec_in)
        outs.append(out)
        gins.append(gin)
        grads = [g.astype(f32) for g in grads]
        sums = grads if sums is None else [s + g for s, g in zip(sums, grads)]
    attn_c, ffn_c = from_places(sums[0]), from_places(sums[1])
    pad_a = attn_params.shape[0] * devices - ATT_MAT - ATT_VEC
    pad_f = ffn_params.shape[0] * devices - FFN_MAT - FFN_VEC
    attn_terms = jnp.concatenate(
        [qkv_flat(attn_c[:24]), tiled_flat(attn_c[24:], 96, 6), sums[2][:30].reshape(-1), jnp.zeros((pad_a,), f32)]
    )
    ffn_terms = jnp.concatenate(
        [
            tiled_flat(ffn_c[:16], 48, 24),
            tiled_flat(ffn_c[16:], 192, 6),
            sums[2][32:74].reshape(-1),
            jnp.zeros((pad_f,), f32),
        ]
    )
    attn_grad = lax.psum_scatter(attn_terms, AXES, scatter_dimension=0, tiled=True)
    ffn_grad = lax.psum_scatter(ffn_terms, AXES, scatter_dimension=0, tiled=True)
    return jnp.stack(outs), jnp.stack(gins), attn_grad, ffn_grad


def solution(mesh):
    linked = tuple(mesh.shape[a] for a in AXES) == (8, 4)
    return jax.shard_map(
        shards_linked if linked else shards_any,
        mesh=mesh,
        in_specs=(P(AXES, None, None), P(AXES), P(AXES), P(AXES), P(AXES, None, None)),
        out_specs=(P(AXES, None, None), P(AXES, None, None), P(AXES), P(AXES)),
        check_vma=False,
    )
```

time: 1170 us -> 554 us (0.47)
  waiting for transfers between devices: 672 us -> 275 us
  matrix products: 239 us -> 0 us
  local copies, waits for them, and re-layouts: 190 us -> 22.5 us
  Pallas kernels: 0 us -> 155 us
  blocking collectives: 0 us -> 43.2 us
    unnamed x4 -> x2, waiting for transfers between devices: 672 us -> 0.03 us
    reduce_scatter x0 -> x2, waiting for transfers between devices: none -> 272 us  [scatter(): lax.psum_scatter(chunks.astype(f32), AXES, scatter_dimension=0, tiled=True)]
    dot_general x96 -> x0, matrix products: 239 us -> none  [the longest x40 84.8 us: contract_cols(): lax.dot_general(left, right, (((1,), (1,)), ((), ())), preferred_element_...]
    pallas_call x0 -> x1, Pallas kernels: none -> 155 us  [run_layer(): pl.pallas_call(body, out_shape=(jax.ShapeDtypeStruct((R, D), bf16), jax.S...]
    unnamed x98 -> x8, local copies, waits for them, and re-layouts: 61.9 us -> 2.78 us
    reshape x10, local copies, waits for them, and re-layouts: 49.5 us -> 1.91 us  [the longest x1 0.79 us: pack_vectors(): ffn_vec.reshape(42, 128)]
    psum x0 -> x1, blocking collectives: none -> 43.2 us  [shards_linked(): ga, gfn, vsum = (scatter(attn_g), scatter(ffn_g), lax.psum(vg, AXES))]
    dynamic_slice x36 -> x0, local copies, waits for them, and re-layouts: 23.2 us -> none  [the longest x24 14.1 us: shards(): mixed_heads, log_total = lax.map(attend, (query, keys, values, head_len))]
  transfers between devices with their start and end apart: 2 -> 4, of which waited for: 2 -> 3; matrix products, arithmetic and copies ran while one was open for 1% -> 6% of each run, Pallas kernels for 0% -> 0%
where the time goes in v1:
time: 554 us; the launch traced here: 553 us
  waiting for transfers between devices  275 us (50%)
  Pallas kernels  155 us (28%)
  blocking collectives  43.2 us (8%)
  other arithmetic  34.7 us (6%)
  local copies, waits for them, and re-layouts  22.5 us (4%)
  between operations  15 us (3%)
  starting transfers between devices  8.39 us (2%)
    reduce_scatter x2, waiting for transfers between devices, scatter(): lax.psum_scatter(chunks.astype(f32), AXES, scatter_dimension=0, tiled=True)  272 us
    pallas_call x1, Pallas kernels, run_layer(): pl.pallas_call(body, out_shape=(jax.ShapeDtypeStruct((R, D), bf16), jax.S...  155 us
    psum x1, blocking collectives, shards_linked(): ga, gfn, vsum = (scatter(attn_g), scatter(ffn_g), lax.psum(vg, AXES))  43.2 us
    convert_element_type x2, other arithmetic, scatter(): chunks.astype(f32)  18.7 us
  transfers between devices with their start and end apart: 4, of which 3 were waited for; matrix products, arithmetic and copies ran while one was open for 6% of the time, Pallas kernels for 0%

profile of v1, /device:TPU:1, one launch (start us, length us, event | category | flops | bytes accessed | tf_op | source)
XLA Modules:
  0.0 553.0 jit_solution(1380711174256009782)
XLA Ops:
  7.2 0.8 slice_bitcast_fusion.3
  8.0 0.8 slice_bitcast_fusion.2
  8.8 4.5 collective-permute-start
  13.5 0.7 maximum_maximum_fusion.args_5_
  14.9 1.1 fusion.3
  16.2 1.3 fusion.2
  17.5 0.1 reshape.52
  17.7 0.7 bitcast_select_fusion.1.args_3_
  18.4 0.8 bitcast_select_fusion.args_4_
  19.1 154.6 %shard_map.84 = (bf16[768,768]{1,0:T(8,128)(2,1)}, bf16[768,768]{1,0:T(8,128)(2,1)}, bf16[4,2,4,576,128]{4,3,2,1,0:T(8,128)(2,1)}, bf16[4,2,4,1152,128]{4,3,2,1,0:T(8,128)(2,1)}, f32[80,128]{1,0:T(8,128)}) custom-call(s32[1]{0:T(128)S(6)} %copy.35.args_0_, bf16[768,768]{1,0:T(8,128)(2,1)} %bitcast.80, bf16[768,768]{1,0:T(8,128)(2,1)} %bitcast.81, ...), custom_call_target="tpu_custom_call" | custom-call | tf_op jit(solution)/shard_map/pallas_call | solution.py:707
  173.8 2.7 fusion.5
  176.5 0.2 copy.29
  176.6 0.4 pad_maximum_fusion.1
  177.1 5.1 bitcast_convert_fusion.1
  182.3 7.0 %fusion.4 = (bf16[4,1,4,1152,128]{4,3,2,1,0:T(8,128)(2,1)S(1)}, bf16[4,1,4,1152,128]{4,3,2,1,0:T(8,128)(2,1)}) fusion(bf16[4,2,4,1152,128]{4,3,2,1,0:T(8,128)(2,1)} %get-tuple-element.13), kind=kLoop, calls=%fused_computation.33 | loop fusion | bytes 18874368 | tf_op jit(solution)/shard_map/slice | solution.py:771
  189.3 2.5 copy.28
  191.8 8.7 %pad_maximum_fusion = bf16[4,2,2,2,1152,128]{5,4,3,2,1,0:T(8,128)(2,1)} fusion(bf16[4,2,2,1,1152,128]{5,4,3,2,1,0:T(8,128)(2,1)} %bitcast.68, bf16[4,2,2,1,1152,128]{5,4,3,2,1,0:T(8,128)(2,1)} %bitcast.67), kind=kLoop, calls=%fused_computation | loop fusion | flops 4718592 | bytes 18874368 | tf_op jit(solution)/shard_map/stack | solution.py:773
  200.6 13.5 %bitcast_convert_fusion = f32[32,1152,128]{2,1,0:T(8,128)} fusion(bf16[4,2,2,2,1152,128]{5,4,3,2,1,0:T(8,128)(2,1)} %pad_maximum_fusion), kind=kLoop, calls=%fused_computation.1 | loop fusion | flops 4718592 | bytes 28311552 | tf_op jit(solution)/shard_map/convert_element_type | solution.py:774
  214.1 0.7 copy-done.2
  214.9 43.2 %psum.7 = f32[80,128]{1,0:T(8,128)S(1)} all-reduce(f32[80,128]{1,0:T(8,128)S(1)} %copy-done.2), channel_id=1, replica_groups=mesh['dp'=8,'fsdp'=4] {'dp','fsdp'}, use_global_device_ids=true, to_apply=%region_1.2 | all-reduce | flops 10240 | bytes 81920 | tf_op jit(solution)/shard_map/psum | solution.py:776
  258.1 60.3 %reduce-scatter.3.cloned.1.call-done = f32[1,576,128]{2,1,0:T(8,128)} async-done(((f32[32,576,128]{2,1,0:T(8,128)}), f32[1,576,128]{2,1,0:T(8,128)}) %reduce-scatter.3.cloned.1.call-update) | async-done | bytes 294928 | tf_op jit(solution)/shard_map/reduce_scatter | solution.py:774
  318.4 1.1 copy.32
  319.6 1.1 copy.31
  320.8 211.6 %reduce-scatter.5.cloned.1.call-done = f32[1,1152,128]{2,1,0:T(8,128)} async-done(((f32[32,1152,128]{2,1,0:T(8,128)}), f32[1,1152,128]{2,1,0:T(8,128)}) %reduce-scatter.5.cloned.1.call-update) | async-done | bytes 589840 | tf_op jit(solution)/shard_map/reduce_scatter | solution.py:774
  532.5 1.4 copy.30
  534.0 1.4 copy.22
  535.5 3.8 collective-permute-start.1
  539.3 2.7 collective-permute-done.1
  542.0 1.0 fusion.1
  542.9 1.2 fusion
  544.2 1.0 copy.36
  545.2 1.0 copy.37
  (36 shorter events, 0.8 us)
Async XLA Ops:
  7.2 311.2 %reduce-scatter.3.cloned.1.call-start = ((), (), s32[]{:S(2)}) async-start(), calls=%async_computation.2 | async-start | bytes 9732096 | tf_op jit(solution)/shard_map/reduce_scatter | solution.py:774
  8.8 6.1 %collective-permute-start = (bf16[9216]{0:T(1024)(128)(2,1)S(1)}, bf16[9216]{0:T(1024)(128)(2,1)S(1)}, u32[]{:S(2)}, u32[]{:S(2)}) collective-permute-start(bf16[9216]{0:T(1024)(128)(2,1)S(1)} %pad_maximum_fusion.3), channel_id=1, source_target_pairs={{0,1},{1,2},{2,3},{3,4},{4,5},{5,6},{6,7},{7,8},{8,9},{9,10},{10,1... | collective-permute-start | bytes 55304 | tf_op jit(solution)/shard_map/ppermute | solution.py:758
  182.2 350.2 %reduce-scatter.5.cloned.1.call-start = ((), (), s32[]{:S(2)}) async-start(), calls=%async_computation.3 | async-start | bytes 19464192 | tf_op jit(solution)/shard_map/reduce_scatter | solution.py:774
  214.1 0.8 copy-start.2
  533.9 11.3 %copy-start = (bf16[768,768]{1,0:T(8,128)(2,1)S(1)}, bf16[768,768]{1,0:T(8,128)(2,1)}, u32[]{:S(2)}) copy-start(bf16[768,768]{1,0:T(8,128)(2,1)} %get-tuple-element.10) | copy-start | bytes 3538948
  534.0 10.2 %copy-start.1 = (bf16[768,768]{1,0:T(8,128)(2,1)S(1)}, bf16[768,768]{1,0:T(8,128)(2,1)}, u32[]{:S(2)}) copy-start(bf16[768,768]{1,0:T(8,128)(2,1)} %get-tuple-element.9) | copy-start | bytes 3538948
  535.5 6.4 %collective-permute-start.1 = (f32[9216]{0:T(1024)S(1)}, f32[9216]{0:T(1024)S(1)}, u32[]{:S(2)}, u32[]{:S(2)}) collective-permute-start(f32[9216]{0:T(1024)S(1)} %pad_maximum_fusion.2), channel_id=1, source_target_pairs={{1,0},{2,1},{3,2},{4,3},{5,4},{6,5},{7,6},{8,7},{9,8},{10,9},{11,1... | collective-permute-start | bytes 110600 | tf_op jit(solution)/shard_map/ppermute | solution.py:781
Sparse Core Ops, SparseCore 0:
  182.4 135.9 reduce-scatter.2
  325.9 206.4 reduce-scatter.4

commit v2 on v1

--- a/solution.py
+++ b/solution.py
@@ -75,6 +75,18 @@
             attn[z, c, s, pl.ds(pl.multiple_of(i * 96 + 32 * p, 32), 32), :] = value[
                 32 * d : 32 * d + 32, 128 * p : 128 * p + 128
             ]
+
+
+def w_qkv_rows(attn, chunks, part):
+    return jnp.concatenate(
+        [
+            jnp.concatenate(
+                [block(attn, d, slice(96 * i + 32 * part, 96 * i + 32 * part + 32)) for i in range(PAIRS)], axis=1
+            )
+            for d in chunks
+        ],
+        axis=0,
+    )
 
 
 def w_out_cols(attn, j):
@@ -221,20 +233,33 @@
 BLOCKS = R // ROWS
 
 
-def layer_kernel(gather, refs):
+def layer_kernel(gather, scatter, refs):
     length = refs["length"][0]
-    x, cot = refs["x"], refs["cot"]
+    x, io = refs["x"], refs["io"]
+
+    def cot_copy(b):
+        slot = lax.rem(b, 2)
+        return pltpu.make_async_copy(refs["cot"].at[aligned(b * ROWS, ROWS)], refs["cot_b"].at[slot], io.at[6 + slot])
+
+    def out_copy(b):
+        slot = lax.rem(b, 2)
+        return pltpu.make_async_copy(refs["out_b"].at[slot], refs["out"].at[aligned(b * ROWS, ROWS)], io.at[8 + slot])
+
+    x_copy = pltpu.make_async_copy(refs["x_in"], x, io.at[0])
+    x_copy.start()
+    cot_copy(0).start()
     attn, ffn, vec, vg = refs["attn"], refs["ffn"], refs["vec"], refs["vg"]
-    qx, kk, vv, mix = refs["qx"], refs["k"], refs["v"], refs["mix"]
+    qx, kk, vv = refs["qx"], refs["k"], refs["v"]
     xh1, rs1, n1 = refs["xh1"], refs["rs1"], refs["n1"]
-    act, gp, r2, gf, do = refs["act"], refs["gp"], refs["r2"], refs["gf"], refs["do"]
-    out, gin = refs["out"], refs["gin"]
+    act, gp, r2, gf = refs["act"], refs["gp"], refs["r2"], refs["gf"]
+    do, mix = n1, refs["mix"]
 
     def dead_keys():
         row = lax.broadcasted_iota(jnp.int32, (R, 128), 0)
         return jnp.where(row < length, 0.0, -1e30).astype(bf16)
 
     gather.start()
+    x_copy.wait()
 
     def forward_pair(i, carry):
         gather.before_pair(i)
@@ -254,7 +279,7 @@
         return carry
 
     lax.fori_loop(0, PAIRS, forward_pair, 0)
-    gather.step("out")
+    gather.step(0)
     for j in range(3):
         cols = slice(256 * j, 256 * j + 256)
         xh1[:, cols] = nn(mix[...], w_out_cols(attn, j)) + wide(vec, B_OUT + 2 * j, 2) + x[:, cols].astype(f32)
@@ -270,8 +295,8 @@
         n1[rows, :] = (xhat * wide(vec, G1) + wide(vec, B1)).astype(bf16)
         return carry
 
+    gather.step(1)
     lax.fori_loop(0, BLOCKS, norm1, 0)
-    gather.step("norm1")
 
     def ffn_in(j, carry):
         gather.before_in(j)
@@ -304,10 +329,15 @@
         cen = r - jnp.mean(r, axis=-1, keepdims=True)
         rstd = lax.rsqrt(jnp.mean(cen * cen, axis=-1, keepdims=True) + 1e-05)
         xhat = cen * rstd
+        pl.when(b + 1 < BLOCKS)(lambda: cot_copy(b + 1).start())
+        cot_copy(b).wait()
+        pl.when(b >= 2)(lambda: out_copy(b - 2).wait())
         row = lax.broadcasted_iota(jnp.int32, (ROWS, D), 0) + b * ROWS
         valid = jnp.where(row < length, 1.0, 0.0)
-        out[rows, :] = ((xhat * wide(vec, G2) + wide(vec, B2)) * valid).astype(bf16)
-        g = cot[rows, :].astype(f32) * valid
+        slot = lax.rem(b, 2)
+        refs["out_b"][slot] = ((xhat * wide(vec, G2) + wide(vec, B2)) * valid).astype(bf16)
+        out_copy(b).start()
+        g = refs["cot_b"][slot].astype(f32) * valid
         grad = norm_back(g, xhat, wide(vec, G2), rstd)
         r2[rows, :] = grad
         low = grad.astype(bf16)
@@ -316,11 +346,14 @@
 
     zeros = jnp.zeros((1, D), f32)
     d_g2, d_b2, d_bfc = lax.fori_loop(0, BLOCKS, norm2, (zeros, zeros, zeros))
+    for b in (BLOCKS - 2, BLOCKS - 1):
+        out_copy(b).wait()
     put_wide(vg, G2, d_g2)
     put_wide(vg, B2, d_b2)
     put_wide(vg, B_FC, d_bfc)
 
     def back_fc(m, carry):
+        scatter.in_fc(m)
         cols = aligned(m * 384, 384)
         grad_act = nt(gf[...], w_fc_rows(ffn, m))
         low = (grad_act * gp[:, cols].astype(f32)).astype(bf16)
@@ -334,6 +367,7 @@
     lax.fori_loop(0, 8, back_fc, 0)
 
     def back_in(j, carry):
+        scatter.in_in(j)
         cols = aligned(j * 512, 512)
         g = gp[:, cols]
         r2[...] += nt(g, w_in_cols(ffn, j, 4))
@@ -341,6 +375,7 @@
         return carry
 
     lax.fori_loop(0, 6, back_in, 0)
+    scatter.between(0)
 
     def back_norm1(b, sums):
         rows = aligned(b * ROWS, ROWS)
@@ -355,11 +390,13 @@
     put_wide(vg, G1, d_g1)
     put_wide(vg, B1, d_b1)
     put_wide(vg, B_OUT, d_bout)
+    scatter.between(1)
 
     for half in range(2):
         do[:, 384 * half : 384 * half + 384] = nt(
             gf[...], w_out_rows(attn, range(24 + 4 * half, 28 + 4 * half))
         ).astype(bf16)
+    scatter.between(2)
     for half in range(2):
         cols = slice(384 * half, 384 * half + 384)
         grad = tn(mix[:, cols], gf[...]).astype(bf16)
@@ -369,19 +406,36 @@
                 attn[z, c, s, 96 * j : 96 * j + 96, :] = grad[96 * d : 96 * d + 96, 128 * j : 128 * j + 128]
 
     def backward_pair(i, carry):
+        scatter.pair_start(i)
         lane = lane_ids()
         cols = aligned(i * 128, 128)
         q_aug = [qx[:, pl.ds(pl.multiple_of(i * 256 + 128 * h, 128), 128)] for h in range(2)]
-        dq, dk, dv = attend_pair_back(q_aug, kk[:, cols], vv[:, cols], do[:, cols], mix[:, cols], dead_keys(), lane)
+        dq, dk, dv = attend_pair_back(
+            q_aug, kk[:, cols], vv[:, cols], do[:, cols], mix[:, cols], dead_keys(), lane
+        )
+        do[:, cols] = dq
+        kk[:, cols] = dk
+        vv[:, cols] = dv
+        scatter.pair_end(i)
         vg[pl.ds(B_Q + i, 1), :] = column_sum(dq)
         vg[pl.ds(B_V + i, 1), :] = column_sum(dv)
-        grad = jnp.concatenate([dq, dk, dv], axis=1)
-        r2[...] += nt(grad, w_qkv_pair(attn, i))
-        put_w_qkv_pair(attn, i, tn(x[...], grad).astype(bf16))
+        put_w_qkv_pair(refs["qkv_g"], i, tn(x[...], jnp.concatenate([dq, dk, dv], axis=1)).astype(bf16))
         return carry
 
     lax.fori_loop(0, PAIRS, backward_pair, 0)
-    gin[...] = r2[...].astype(bf16)
+    gin_copies = []
+    for n in range(3):
+        scatter.tail(n)
+        cols = slice(256 * n, 256 * n + 256)
+        total = r2[:, cols]
+        for p, g in enumerate((do, kk, vv)):
+            total = total + nt(g[...], w_qkv_rows(attn, range(8 * n, 8 * n + 8), p))
+        mix[:, cols] = total.astype(bf16)
+        gin_copies.append(pltpu.make_async_copy(mix.at[:, cols], refs["gin"].at[:, cols], io.at[1 + n]))
+        gin_copies[-1].start()
+    scatter.tail(3)
+    for copy in gin_copies:
+        copy.wait()
 
 
 class Loaded:
@@ -391,8 +445,8 @@
     def start(self):
         r = self.refs
         copies = [
-            pltpu.make_async_copy(r["attn_in"], r["attn"], r["sems"].at[0]),
-            pltpu.make_async_copy(r["ffn_in"], r["ffn"], r["sems"].at[1]),
+            pltpu.make_async_copy(r["attn_in"], r["attn"], r["io"].at[8]),
+            pltpu.make_async_copy(r["ffn_in"], r["ffn"], r["io"].at[9]),
         ]
         for c in copies:
             c.start()
@@ -424,13 +478,93 @@
     )
 
 
-GROUPS = 10
+ATT_GROUPS = (192, 192, 192)
+FFN_GROUPS = (192, 96, 288, 288, 288)
+PLANE_GROUPS = 2
+Z, PASS, A, B, C, HOP = range(1, 7)
+VECTOR_MARKS = (3003, 4003, 5003)
+GATHER_ENDS = {
+    0: (3030, 3040, 1000, 1010, 1020, 1050, 3000, 3010, 3020, 3050, 3060, 3070, 4030, 4040, 3001, 4000, 4010, 4020, 3011, 4050, 3002, 3021, 6030, 6040, 1060, 1070, 4060, 4070, 3003, 5000, 3012, 4001, 4011, 5010, 4002, 3022, 4021, 5020, 4003, 6031, 4012, 4022, 5050, 6041, 3013, 5060, 3023, 5070, 3051, 4013, 5001, 4023, 3061, 5011, 4051, 5002, 3071, 3052, 4061, 5021, 3053, 5003,),
+    2: (5012, 4052, 4071, 3062,),
+    4: (6032, 5013, 5022, 4053, 5023,),
+    6: (6042, 5051, 4062, 3072, 3063,),
+    8: (5052, 5061, 3073,),
+    10: (4072,),
+    12: (5071, 4063, 4073,),
+    13: (5053, 5062,),
+    14: (6033, 5063, 6043, 5072,),
+    15: (5073,),
+}
+GATHER_MIDDLE = {
+    0: (3030, 3040, 1000, 1010, 1020, 3000, 3010, 3020, 3050, 3060, 3070, 4030, 4040, 3001, 3002, 4000, 4010, 4020, 2003, 3003, 3011, 4050, 6030, 3012, 6040, 4060, 2013, 3013, 3021, 4070, 5000, 3022, 4001, 4002, 5010, 2023, 1050, 1060, 1070, 4003, 3023, 4011, 5020, 3051, 4012, 4013, 4021, 2053, 5050, 3053, 4022, 6032, 4023, 5060, 6042, 6031, 4051, 3052, 4053, 6041, 5070, 5001, 3061, 5002, 4052, 5003, 3062, 4061, 2063, 3063,),
+    2: (5011, 5012, 3071,),
+    4: (5013, 2073, 4062, 4063, 5021, 3072, 3073,),
+    6: (5022, 4071,),
+    8: (5023, 4072, 4073, 5051,),
+    10: (6033, 5053,),
+    12: (6043, 5052, 5061,),
+    13: (5062, 5063,),
+    14: (5071,),
+    15: (5072,),
+    17: (5073,),
+}
+SCATTER = {
+    4: (100, 101, 102, 103,),
+    5: (200,),
+    6: (201, 202, 203,),
+    8: (300, 104, 105, 106, 107,),
+    9: (301, 204, 205, 108,),
+    10: (302, 206, 207, 400, 208, 109,),
+    11: (401, 303, 209, 110,),
+    12: (402, 210, 111,),
+    13: (304, 211, 403, 112,),
+    14: (305, 212, 113, 500,),
+    15: (404, 306, 213, 405, 307,),
+    16: (501,),
+    17: (114,),
+    19: (502, 406, 308, 407, 214,),
+    20: (503, 309, 115,),
+    22: (408, 310, 215, 504,),
+    23: (116,),
+    25: (409, 410, 311, 216, 505,),
+    26: (312, 117,),
+    28: (411, 313, 217,),
+    29: (506, 118,),
+    31: (508, 412, 413, 218, 314, 509,),
+    32: (507, 119,),
+    34: (315, 316, 219, 510,),
+    35: (414, 120,),
+    36: (317, 220,),
+    37: (511, 415, 318,),
+    38: (416, 512, 417, 319, 418, 320, 419, 513, 420, 514, 515, 516, 517, 518, 519, 520,),
+}
+
+
+ATT, FFN = 0, 1
+
+
+def group_of(g):
+    if g < len(ATT_GROUPS):
+        return ATT, pl.ds(sum(ATT_GROUPS[:g]), ATT_GROUPS[g])
+    g -= len(ATT_GROUPS)
+    return FFN, pl.ds(sum(FFN_GROUPS[:g]), FFN_GROUPS[g])
+
+
+ATT_HEAD, FFN_HEAD = 30, 42
+
+N_GROUPS = len(ATT_GROUPS) + len(FFN_GROUPS)
+PLANE_ROWS = sum(FFN_GROUPS[:PLANE_GROUPS])
+
+
+def is_plane_group(g):
+    return len(ATT_GROUPS) <= g < len(ATT_GROUPS) + PLANE_GROUPS
 
 
 class Gather:
     def __init__(self, refs):
         self.refs = refs
         self.z, self.x, self.y, self.c = z, x, y, c = position()
+        self.me = z * 8 + x * 4 + y * 2 + c
         first = c == 0
         a, b = jnp.where(first, x, y), jnp.where(first, y, x)
         self.slot, self.pair = b * 2 + a, b * 2
@@ -440,223 +574,592 @@
         self.dev_c = device(z, x, y, 1 - c)
         self.zs = [lax.rem(z + k, 4) for k in (1, 2, 3)]
         self.dev_z = [device(t, x, y, c) for t in self.zs]
+        upper = lax.div(z, 2)
+        self.near = [z, z + 1 - 2 * lax.rem(z, 2), 2 - upper, 3 - 3 * upper]
+        self.dev_near = [device(t, x, y, c) for t in self.near]
+        self.is_end = (z == 0) | (z == 3)
+        self.is_middle = (z == 1) | (z == 2)
+        self.from_me = 2 + jnp.where(self.is_end, 1, 0)
+        self.half = upper * 2
+        self.other_half = 2 - upper * 2
+        last = lax.rem(self.me + 1, 32)
+        before = lax.rem(self.me + 31, 32)
+        self.dev_after = (lax.div(last, 4), lax.rem(last, 4))
+        self.dev_before = (lax.div(before, 4), lax.rem(before, 4))
+        self.buf = (refs["attn"], refs["ffn"])
 
     def barrier(self):
         bar = pltpu.get_barrier_semaphore()
-        targets = [self.dev_a, self.dev_b, self.dev_c] + self.dev_z
+        targets = [self.dev_a, self.dev_b, self.dev_c, self.dev_after, self.dev_before] + self.dev_z
         for t in targets:
             pl.semaphore_signal(bar, inc=1, device_id=t, device_id_type=MESH)
         pl.semaphore_wait(bar, len(targets))
 
-    def part(self, g):
-        if isinstance(g, int) and g >= PAIRS:
-            n = g - PAIRS
-            return self.refs["ffn"], (slice(0, 2) if n < 2 else slice(2, 4)), slice(576 * (n % 2), 576 * (n % 2) + 576)
-        return self.refs["attn"], slice(0, 4), aligned(g * 96, 96)
-
-    def send_z(self, g):
-        buf, zz, rows = self.part(g)
-        own = self.refs["own_a"] if buf is self.refs["attn"] else self.refs["own_f"]
+    def z_copy(self, g, k):
+        kind, rows = group_of(g)
+        ref = self.buf[kind].at[self.z, self.c, self.slot, rows]
+        index = 1 if k == 1 else self.from_me
         r = self.refs
-
-        def go():
-            dst = buf.at[self.z, self.c, self.slot, rows]
-            pltpu.make_async_copy(own.at[rows], dst, r["own_sem"].at[g]).start()
-            for k in range(3):
-                remote(own.at[rows], dst, r["zs"].at[g, k], r["zr"].at[g, k], self.dev_z[k]).start()
-
-        self.if_in(zz, go)
-
-    def if_in(self, zz, fn):
-        if zz == slice(0, 4):
-            fn()
+        return remote(ref, ref, r["gs"].at[8 + 3 * kind + k - 1], r["zr"].at[g, index], self.dev_near[k])
+
+    def pass_copy(self, g):
+        kind, rows = group_of(g)
+        ref = self.buf[kind].at[self.near[3], self.c, self.slot, rows]
+        return remote(ref, ref, self.refs["gs"].at[14 + kind], self.refs["zr"].at[g, 3], self.dev_near[1])
+
+    def z_arrival(self, g, k):
+        kind, rows = group_of(g)
+        wide_ = pl.ds(0, 4) if is_plane_group(g) else self.slot
+        ref = self.buf[kind].at[self.near[k], self.c, wide_, rows]
+        return remote(ref, ref, self.refs["gs"].at[8], self.refs["zr"].at[g, k], self.dev_near[1])
+
+    def hop_copy(self, g, k, n):
+        _, rows = group_of(g)
+        layer = self.near[max(n - 1, 0)]
+        ref = self.refs["ffn"].at[layer, self.c, :, rows]
+        target = self.dev_near[2 if n in (1, 2) else 1]
+        index = (1, 2, 3, 2, 3)[n]
+        return remote(ref, ref, self.refs["gs"].at[16 + n], self.refs["zr"].at[g, index], target)
+
+    def plane_copy(self, step, g, k):
+        kind, rows = group_of(g)
+        r = self.refs
+        at = self.buf[kind].at[self.near[k], self.c]
+        later = 0 if kind == ATT else 1 if k == 0 else 2
+        if step == A:
+            src, send, recv, target = at.at[self.slot, rows], later, "ar", self.dev_a
+        elif step == B:
+            src, send, recv, target = at.at[pl.ds(self.pair, 2), rows], 3 + later, "br", self.dev_b
         else:
-            pl.when((self.z >= zz.start) & (self.z < zz.stop))(fn)
-
-    def relay_a(self, g):
-        buf, zz, rows = self.part(g)
+            src, send, recv, target = at.at[:, rows], 6 + kind, "cr", self.dev_c
+        return remote(src, src, r["gs"].at[send], r[recv].at[g, k], target)
+
+    def run(self, code):
+        kind, g, k = code // 1000, code // 10 % 100, code % 10
+        if kind == Z:
+            self.z_copy(g, 1).start()
+            self.z_copy(g, 2).start()
+            pl.when(self.is_middle)(lambda: self.z_copy(g, 3).start())
+            return
+        if kind == PASS:
+            self.z_arrival(g, 3).wait_recv()
+            self.pass_copy(g).start()
+            return
+        if kind == HOP:
+            if k == 0:
+                self.plane_copy(B, g, 0).wait_recv()
+                self.hop_copy(g, 0, 0).start()
+                pl.when(self.is_middle)(lambda: self.hop_copy(g, 0, 1).start())
+            else:
+                self.z_arrival(g, k).wait_recv()
+                pl.when(self.is_middle)(lambda: self.hop_copy(g, k, k + 1).start())
+            self.plane_copy(C, g, k).start()
+            return
+        if kind == A and k in (1, 2):
+            self.z_arrival(g, k).wait_recv()
+        elif kind == A and k == 3:
+            pl.when(self.is_end)(lambda: self.z_arrival(g, 3).wait_recv())
+        elif kind == B:
+            self.plane_copy(A, g, k).wait_recv()
+        elif kind == C:
+            self.plane_copy(B, g, k).wait_recv()
+        self.plane_copy(kind, g, k).start()
+
+    def ready(self, g, first, count):
+        kind, rows = group_of(g)
         r = self.refs
-        one = buf.at[self.z, self.c, self.slot, rows]
-        own = self.refs["own_a"] if buf is self.refs["attn"] else self.refs["own_f"]
-        self.if_in(zz, lambda: pltpu.make_async_copy(own.at[rows], one, r["own_sem"].at[g]).wait())
-        for k in range(3):
-            source = lax.rem(self.z + 3 - k, 4)
-
-            def got(k=k, source=source):
-                dst = buf.at[source, self.c, self.slot, rows]
-                remote(dst, dst, r["zs"].at[g, k], r["zr"].at[g, k], self.dev_z[k]).wait_recv()
-
-            if zz == slice(0, 4):
-                got()
-            else:
-                pl.when((source >= zz.start) & (source < zz.stop))(got)
-        mine = buf.at[zz, self.c, self.slot, rows]
-        remote(mine, mine, r["as"].at[g], r["ar"].at[g], self.dev_a).start()
-
-    def relay_b(self, g):
-        buf, zz, rows = self.part(g)
-        r = self.refs
-        got = buf.at[zz, self.c, self.other_slot, rows]
-        remote(got, got, r["as"].at[g], r["ar"].at[g], self.dev_a).wait_recv()
-        mine = buf.at[zz, self.c, pl.ds(self.pair, 2), rows]
-        remote(mine, mine, r["bs"].at[g], r["br"].at[g], self.dev_b).start()
-
-    def relay_c(self, g):
-        buf, zz, rows = self.part(g)
-        r = self.refs
-        got = buf.at[zz, self.c, pl.ds(self.other_pair, 2), rows]
-        remote(got, got, r["bs"].at[g], r["br"].at[g], self.dev_b).wait_recv()
-        mine = buf.at[zz, self.c, :, rows]
-        remote(mine, mine, r["cs"].at[g], r["cr"].at[g], self.dev_c).start()
-
-    def ready(self, g):
-        buf, zz, rows = self.part(g)
-        r = self.refs
-        got = buf.at[zz, 1 - self.c, :, rows]
-        remote(got, got, r["cs"].at[g], r["cr"].at[g], self.dev_c).wait_recv()
+        for n in range(count):
+            ref = self.buf[kind].at[0, 1 - self.c, :, rows]
+            remote(ref, ref, r["gs"].at[6 + kind], r["cr"].at[g, first + n], self.dev_c).wait_recv()
+
+    def steps(self, key):
+        for who, table in ((self.is_end, GATHER_ENDS), (self.is_middle, GATHER_MIDDLE)):
+            if key in table:
+
+                @pl.when(who)
+                def _(table=table):
+                    for s in table[key]:
+                        self.run(s)
 
     def vectors(self, stage):
         r = self.refs
-        buf, own = r["vec_all"], r["own_v"]
+        buf, own, v = r["vec_all"], r["tail"], r["vsem"]
         one = buf.at[self.c, self.slot]
         if stage == 0:
 
             @pl.when(self.z == 3)
             def _():
-                pltpu.make_async_copy(own, one, r["vsem"].at[0]).start()
+                one[...] = own[...]
                 for k in range(3):
-                    remote(own, one, r["vsem"].at[4 + k], r["vsem"].at[1], self.dev_z[k]).start()
+                    remote(own, one, v.at[4 + k], v.at[1], self.dev_z[k]).start()
 
         elif stage == 1:
 
             @pl.when(self.z == 3)
             def _():
-                pltpu.make_async_copy(own, one, r["vsem"].at[0]).wait()
                 for k in range(3):
-                    remote(own, one, r["vsem"].at[4 + k], r["vsem"].at[1], self.dev_z[k]).wait_send()
+                    remote(own, one, v.at[4 + k], v.at[1], self.dev_z[k]).wait_send()
 
             @pl.when(self.z != 3)
             def _():
-                remote(one, one, r["vsem"].at[4], r["vsem"].at[1], self.dev_z[0]).wait_recv()
-
-            remote(one, one, r["vsem"].at[7], r["vsem"].at[2], self.dev_a).start()
+                remote(one, one, v.at[4], v.at[1], self.dev_z[0]).wait_recv()
+
+            remote(one, one, v.at[7], v.at[2], self.dev_a).start()
         elif stage == 2:
             got = buf.at[self.c, self.other_slot]
-            remote(got, got, r["vsem"].at[7], r["vsem"].at[2], self.dev_a).wait()
+            remote(got, got, v.at[7], v.at[2], self.dev_a).wait()
             mine = buf.at[self.c, pl.ds(self.pair, 2)]
-            remote(mine, mine, r["vsem"].at[8], r["vsem"].at[3], self.dev_b).start()
+            remote(mine, mine, v.at[8], v.at[3], self.dev_b).start()
         elif stage == 3:
             got = buf.at[self.c, pl.ds(self.other_pair, 2)]
-            remote(got, got, r["vsem"].at[8], r["vsem"].at[3], self.dev_b).wait()
+            remote(got, got, v.at[8], v.at[3], self.dev_b).wait()
             mine = buf.at[self.c]
-            remote(mine, mine, r["vsem"].at[9], r["vsem"].at[10], self.dev_c).start()
+            remote(mine, mine, v.at[9], v.at[10], self.dev_c).start()
         else:
             got = buf.at[1 - self.c]
-            remote(got, got, r["vsem"].at[9], r["vsem"].at[10], self.dev_c).wait()
+            remote(got, got, v.at[9], v.at[10], self.dev_c).wait()
             r["vec"][...] = buf[1, 3].astype(f32)
 
+    def tail_copy(self):
+        t = self.refs["tail"]
+        return remote(t, self.refs["tail_in"], self.refs["vsem"].at[11], self.refs["vsem"].at[12], self.dev_after)
+
+    def load_own(self):
+        r = self.refs
+        flat_a, flat_f = r["flat_a"], r["flat_f"]
+        own_a, own_f = r["attn_own"], r["ffn_own"]
+        whole_a, whole_f = ATT_ROWS * 128, FFN_ROWS * 128
+        flat_a[ATT_HEAD + ATT_ROWS : ATT_HEAD + ATT_ROWS + 16, :] = jnp.zeros((16, 128), f32)
+        flat_f[FFN_HEAD + FFN_ROWS : FFN_HEAD + FFN_ROWS + 16, :] = jnp.zeros((16, 128), f32)
+        flat_a[pl.ds(ATT_HEAD, ATT_ROWS), :] = own_a[0:whole_a].reshape(ATT_ROWS, 128).astype(f32)
+        flat_f[pl.ds(FFN_HEAD, FFN_ROWS), :] = own_f[0:whole_f].reshape(FFN_ROWS, 128).astype(f32)
+        at = ATT_HEAD + ATT_ROWS
+        flat_a[at : at + 1, 0:120] = own_a[whole_a : whole_a + 120].reshape(1, 120).astype(f32)
+        at = FFN_HEAD + FFN_ROWS
+        flat_f[at : at + 1, :] = own_f[whole_f : whole_f + 128].reshape(1, 128).astype(f32)
+        flat_f[at + 1 : at + 2, 0:40] = own_f[whole_f + 128 : whole_f + 168].reshape(1, 40).astype(f32)
+        lane = lax.broadcasted_iota(jnp.int32, (32, 128), 1)
+        v = pltpu.roll(flat_a[ATT_HEAD + 546 : ATT_HEAD + 586, :], 8, 1)
+        r["tail"][0:32, :] = jnp.where(lane < 8, v[0:32], v[1:33]).astype(bf16)
+        lane = lax.broadcasted_iota(jnp.int32, (48, 128), 1)
+        v = pltpu.roll(flat_f[FFN_HEAD + 1111 : FFN_HEAD + 1167, :], 88, 1)
+        r["tail"][32:80, :] = jnp.where(lane < 88, v[0:48], v[1:49]).astype(bf16)
+
+    def place_own(self, kind):
+        r = self.refs
+        if kind == ATT:
+            flat, rows, head, size, moved, at = r["flat_a"], r["rows_a"], ATT_HEAD, ATT_ROWS, 120, 0
+        else:
+            flat, rows, head, size, moved, at = r["flat_f"], r["rows_f"], FFN_HEAD, FFN_ROWS, 168, 32
+        flat[0:head, :] = r["tail_in"][at : at + head, :].astype(f32)
+        self.shifted(flat, rows, head * 128 - moved * self.me, size)
+        slot = self.buf[kind].at[self.z, self.c, self.slot]
+        self.by_kind(kind, lambda tiles, n, at: self.to_tiles(rows, slot, tiles, n, at))
+
+    def by_kind(self, kind, fn):
+        if kind == ATT:
+            pl.when(self.z < 3)(lambda: fn(18, 32, lambda t: (t % 6 * 3 + t // 6) * 32))
+            pl.when(self.z == 3)(lambda: fn(6, 96, lambda t: t * 96))
+        else:
+            pl.when(self.z < 2)(lambda: fn(24, 48, lambda t: t * 48))
+            pl.when(self.z >= 2)(lambda: fn(6, 192, lambda t: t * 192))
+
+    def to_tiles(self, rows, slot, tiles, n, at):
+        for t in range(tiles):
+            slot[at(t) : at(t) + n, :] = rows[pl.ds(t, n, stride=tiles), :].astype(bf16)
+
+    def from_tiles(self, total, flat, tiles, n, at):
+        for t in range(tiles):
+            flat[pl.ds(t, n, stride=tiles), :] = total[at(t) : at(t) + n, :]
+
+    def shifted(self, src, dst, shift, count):
+        row, turn = lax.div(shift, 128), lax.rem(shift, 128)
+
+        def step(n, carry):
+            lane = lax.broadcasted_iota(jnp.int32, (64, 128), 1)
+            back = lax.rem(128 - turn, 128)
+            low = pltpu.roll(src[pl.ds(n * 64 + row, 64), :], back, 1)
+            high = pltpu.roll(src[pl.ds(n * 64 + row + 1, 64), :], back, 1)
+            dst[pl.ds(pl.multiple_of(n * 64, 64), 64), :] = jnp.where(lane < 128 - turn, low, high)
+            return carry
+
+        lax.fori_loop(0, count // 64, step, 0)
+
     def start(self):
+        self.load_own()
         self.barrier()
+        pl.when(self.me < 31)(lambda: self.tail_copy().start())
         self.vectors(0)
-        for g in range(GROUPS):
-            self.send_z(g)
-        self.vectors(1)
-        self.relay_a(0)
-        self.vectors(2)
-        self.relay_b(0)
-        self.relay_a(1)
+        pl.when(self.me > 0)(lambda: self.tail_copy().wait_recv())
+        self.place_own(ATT)
+        for g in range(len(ATT_GROUPS)):
+            self.run(1000 * Z + 10 * g)
+        self.place_own(FFN)
+        for who, table in ((self.is_end, GATHER_ENDS), (self.is_middle, GATHER_MIDDLE)):
+
+            @pl.when(who)
+            def _(table=table):
+                first = [v for v in table[0] if v >= 1000 * Z + 10 * len(ATT_GROUPS)]
+                cuts = [0] + [first.index(v) + 1 for v in VECTOR_MARKS] + [len(first)]
+                for stage in range(4):
+                    for s in first[cuts[stage] : cuts[stage + 1]]:
+                        self.run(s)
+                    self.vectors(stage + 1)
+
+    def before_pair(self, i):
+        for v in range(PAIRS):
+
+            @pl.when(i == v)
+            def _(v=v):
+                if v:
+                    self.steps(2 * v)
+                if v * len(ATT_GROUPS) % PAIRS == 0:
+                    self.ready(v * len(ATT_GROUPS) // PAIRS, 0, 4)
+
+    def step(self, n):
+        self.steps(12 + n)
+
+    def before_in(self, j):
+        at = 0
+        for n, rows in enumerate(FFN_GROUPS):
+
+            @pl.when(j == at // 96)
+            def _(n=n):
+                self.steps(14 + n)
+                self.ready(len(ATT_GROUPS) + n, self.half, 2)
+
+            at += rows
+
+    def before_out(self, j):
+        seen = 0
+        for v in range(3):
+            more, at = [], 0
+            for n, rows in enumerate(FFN_GROUPS):
+                if n >= seen and at < 384 * (v + 1):
+                    more.append(n)
+                at += rows
+            seen += len(more)
+
+            @pl.when(j == v)
+            def _(v=v, more=more):
+                self.steps(14 + len(FFN_GROUPS) + v)
+                for n in more:
+                    self.ready(len(ATT_GROUPS) + n, self.other_half, 2)
+
+    def finish(self):
+        self.steps(17 + len(FFN_GROUPS))
+        r = self.refs
+        z, c, gs = self.z, self.c, r["gs"]
+        attn, ffn = self.buf
+        rest = pl.ds(PLANE_ROWS, FFN_ROWS - PLANE_ROWS)
+        front = pl.ds(0, PLANE_ROWS)
+
+        def sent(n, ref):
+            remote(ref, ref, gs.at[n], r["zr"].at[0, 0], self.dev_c).wait_send()
+
+        sent(0, attn.at[:, c, self.slot])
+        sent(1, ffn.at[z, c, self.slot])
+        sent(2, ffn.at[pl.ds(0, 3), c, self.slot, rest])
+        sent(3, attn.at[:, c, pl.ds(self.pair, 2)])
+        sent(4, ffn.at[z, c, pl.ds(self.pair, 2)])
+        sent(5, ffn.at[pl.ds(0, 3), c, pl.ds(self.pair, 2), rest])
+        sent(6, attn.at[:, c])
+        sent(7, ffn.at[:, c])
+        for k in range(2):
+            sent(8 + k, attn.at[z, c, self.slot])
+            sent(11 + k, ffn.at[z, c, self.slot, rest])
+        if PLANE_GROUPS:
+            sent(16, ffn.at[z, c, :, front])
+
+        @pl.when(self.is_middle)
+        def _():
+            sent(10, attn.at[z, c, self.slot])
+            sent(13, ffn.at[z, c, self.slot, rest])
+            sent(14, attn.at[z, c, self.slot])
+            sent(15, ffn.at[z, c, self.slot, rest])
+            if PLANE_GROUPS:
+                for n in range(17, 21):
+                    sent(n, ffn.at[z, c, :, front])
+
+        pl.when(self.me < 31)(lambda: self.tail_copy().wait_send())
+
+
+W_FC, W_IN, W_OUT, W_QKV = 0, 8, 14, 15
+N_ITEMS = W_QKV + PAIRS
+
+
+class Scatter:
+    def __init__(self, refs, gather):
+        self.refs, self.g = refs, gather
+
+    def part(self, item):
+        if item >= W_QKV:
+            return "qkv_g", "attn", range(0, 3), pl.ds(96 * (item - W_QKV), 96), 96, 2
+        if item == W_OUT:
+            return "attn", "attn", range(3, 4), pl.ds(0, 576), 576, 1
+        if item >= W_IN:
+            return "ffn", "ffn", range(0, 2), pl.ds(192 * (item - W_IN), 192), 192, 0
+        z = 2 + item // 4
+        return "ffn", "ffn", range(z, z + 1), pl.ds(288 * (item % 4), 288), 288, 0
+
+    def span(self, zz):
+        return pl.ds(zz[0], len(zz))
+
+    def add(self, pairs, rows, count):
+        def step(n, carry):
+            at = pl.ds(pl.multiple_of(rows.start + n * 96, 96), 96)
+            for dst, src in pairs:
+                d = dst.at[at]
+                d[...] = d[...] + src.at[at][...]
+            return carry
+
+        if count == 96:
+            step(0, 0)
+        else:
+            lax.fori_loop(0, count // 96, step, 0)
+
+    def c_copy(self, g):
+        buf, kind, zz, rows, _, s = self.part(g)
+        r, t = self.refs, self.g
+        return remote(
+            r[buf].at[self.span(zz), 1 - t.c, :, rows],
+            r[kind + "_rc"].at[self.span(zz), :, rows],
+            r["ss"].at[s, 0],
+            r["sr"].at[0, g],
+            t.dev_c,
+        )
+
+    def b_copy(self, g):
+        buf, kind, zz, rows, _, s = self.part(g)
+        r, t = self.refs, self.g
+        return remote(
+            r[buf].at[self.span(zz), t.c, pl.ds(t.other_pair, 2), rows],
+            r[kind + "_rb"].at[self.span(zz), :, rows],
+            r["ss"].at[s, 1],
+            r["sr"].at[1, g],
+            t.dev_b,
+        )
+
+    def a_copy(self, g):
+        buf, kind, zz, rows, _, s = self.part(g)
+        r, t = self.refs, self.g
+        return remote(
+            r[buf].at[self.span(zz), t.c, t.other_slot, rows],
+            r[kind + "_ra"].at[self.span(zz), rows],
+            r["ss"].at[s, 2],
+            r["sr"].at[2, g],
+            t.dev_a,
+        )
+
+    def z_copy(self, g, k):
+        buf, kind, zz, rows, _, s = self.part(g)
+        r, t = self.refs, self.g
+        return remote(
+            r[buf].at[t.zs[k], t.c, t.slot, rows],
+            r[kind + "_rz"].at[k, rows],
+            r["ss"].at[s, 3 + k],
+            r["sr"].at[3, g],
+            t.dev_z[k],
+        )
+
+    def inside(self, value, zz):
+        return (value >= zz[0]) & (value <= zz[-1])
+
+    def c_send(self, g):
+        self.c_copy(g).start()
+
+    def b_send(self, g):
+        buf, kind, zz, rows, n, _ = self.part(g)
+        r, t = self.refs, self.g
+        self.c_copy(g).wait_recv()
+        self.add([(r[buf].at[z, t.c, i], r[kind + "_rc"].at[z, i]) for z in zz for i in range(4)], rows, n)
+        self.b_copy(g).start()
+
+    def a_send(self, g):
+        buf, kind, zz, rows, n, _ = self.part(g)
+        r, t = self.refs, self.g
+        self.b_copy(g).wait_recv()
+        self.add([(r[buf].at[z, t.c, t.pair + i], r[kind + "_rb"].at[z, i]) for z in zz for i in range(2)], rows, n)
+        self.a_copy(g).start()
+
+    def z_send(self, g):
+        buf, kind, zz, rows, n, _ = self.part(g)
+        r, t = self.refs, self.g
+        self.a_copy(g).wait_recv()
+        self.add([(r[buf].at[z, t.c, t.slot], r[kind + "_ra"].at[z]) for z in zz], rows, n)
+        for k in range(3):
+
+            @pl.when(self.inside(t.zs[k], zz))
+            def _():
+                self.z_copy(g, k).start()
+
+    def take(self, g):
+        buf, kind, zz, rows, n, _ = self.part(g)
+        r, t = self.refs, self.g
+
+        @pl.when(self.inside(t.z, zz))
+        def _():
+            got = r[kind + "_rz"].at[:, rows]
+            remote(got, got, r["ss"].at[0, 3], r["sr"].at[3, g], t.dev_c).wait_recv()
+
+            def step(i, carry):
+                at = pl.ds(pl.multiple_of(rows.start + i * 96, 96), 96)
+                total = r[buf][t.z, t.c, t.slot, at, :].astype(f32)
+                for k in range(3):
+                    total = total + r[kind + "_rz"][k, at, :].astype(f32)
+                r[kind + "_sum"][at, :] = total
+                return carry
+
+            lax.fori_loop(0, n // 96, step, 0)
+
+    def vectors(self, stage):
+        r, t = self.refs, self.g
+        own, got, s, v = r["vg"], r["vg_r"], r["vs"], r["vr"]
+        if stage > 0:
+            target = (t.dev_c, t.dev_b, t.dev_a)[stage - 1]
+            remote(own, got.at[stage - 1], s.at[stage - 1], v.at[stage - 1], target).wait()
+            own[...] = own[...] + got[stage - 1]
+        if stage < 3:
+            target = (t.dev_c, t.dev_b, t.dev_a)[stage]
+            remote(own, got.at[stage], s.at[stage], v.at[stage], target).start()
+        else:
+            for k in range(3):
+
+                @pl.when(t.zs[k] == 3)
+                def _():
+                    remote(own, got.at[3 + k], s.at[3 + k], v.at[3 + k], t.dev_z[k]).start()
+
+    def take_vectors(self):
+        r, t = self.refs, self.g
+        own, got, s, v = r["vg"], r["vg_r"], r["vs"], r["vr"]
+        for k in range(3):
+
+            @pl.when(t.zs[k] == 3)
+            def _():
+                remote(own, got.at[3 + k], s.at[3 + k], v.at[3 + k], t.dev_z[k]).wait_send()
+
+        @pl.when(t.z == 3)
+        def _():
+            for k in range(3):
+                remote(own, got.at[3 + k], s.at[3 + k], v.at[3 + k], t.dev_z[k]).wait_recv()
+            own[...] = own[...] + got[3] + got[4] + got[5]
+
+    def sent(self):
+        r, t = self.refs, self.g
+        ss = r["ss"]
+
+        def one(s, n, ref):
+            remote(ref, ref, ss.at[s, n], r["sr"].at[0, 0], t.dev_c).wait_send()
+
+        for s, ref in enumerate((r["ffn"], r["attn"].at[pl.ds(3, 1)], r["qkv_g"])):
+            one(s, 0, ref.at[:, 1 - t.c])
+            one(s, 1, ref.at[:, t.c, pl.ds(t.other_pair, 2)])
+            one(s, 2, ref.at[:, t.c, t.other_slot])
+        for k in range(3):
+            one(0, 3 + k, r["ffn"].at[0, t.c, t.slot])
+            pl.when(t.zs[k] == 3)(lambda k=k: one(1, 3 + k, r["attn"].at[3, t.c, t.slot]))
+            pl.when(t.zs[k] != 3)(lambda k=k: one(2, 3 + k, r["qkv_g"].at[0, t.c, t.slot]))
+
+    def step(self, key):
+        for s in SCATTER.get(key, ()):
+            self.one(s)
+
+    def one(self, s):
+        kinds = (None, self.c_send, self.b_send, self.a_send, self.z_send, self.take)
+        kinds[s // 100](s % 100)
+
+    def loop(self, i, first, stride, count):
+        for v in range(count):
+            if first + stride * v in SCATTER:
+                pl.when(i == v)(lambda v=v: self.step(first + stride * v))
+
+    def in_fc(self, m):
+        self.loop(m, 0, 1, 8)
+
+    def in_in(self, j):
+        self.loop(j, 8, 1, 6)
+
+    def between(self, n):
+        self.step(14 + n)
+
+    def pair_start(self, i):
+        self.loop(i, 17, 3, PAIRS)
+
+    def pair_end(self, i):
+        self.loop(i, 19, 3, PAIRS)
+
+    def tail(self, n):
+        if n < 3:
+            self.step(35 + n)
+            self.vectors(n)
+            return
         self.vectors(3)
-        self.relay_c(0)
-        self.relay_b(1)
-        self.relay_a(2)
-        self.vectors(4)
-
-    def before_pair(self, i):
-        @pl.when(i + 3 < PAIRS)
-        def _():
-            self.relay_a(i + 3)
-
-        @pl.when(i + 2 < PAIRS)
-        def _():
-            self.relay_b(i + 2)
-
-        @pl.when(i + 1 < PAIRS)
-        def _():
-            self.relay_c(i + 1)
-
-        @pl.when(i == 3)
-        def _():
-            self.relay_a(6)
-
-        @pl.when(i == 4)
-        def _():
-            self.relay_b(6)
-
-        @pl.when(i == 5)
-        def _():
-            self.relay_a(7)
-
-        self.ready(i)
-
-    def step(self, name):
-        if name == "out":
-            self.relay_c(6)
-            self.relay_b(7)
-            self.relay_a(8)
-        elif name == "norm1":
-            self.ready(6)
-
-    def before_in(self, j):
-        @pl.when(j == 2)
-        def _():
-            self.relay_c(7)
-            self.relay_b(8)
-            self.relay_a(9)
-
-        @pl.when(j == 6)
-        def _():
-            self.ready(7)
-
-        @pl.when(j == 9)
-        def _():
-            self.relay_c(8)
-            self.relay_b(9)
-
-    def before_out(self, j):
-        @pl.when(j == 0)
-        def _():
-            self.ready(8)
-            self.relay_c(9)
-            self.ready(9)
-
-    def finish(self):
-        r = self.refs
-        for g in range(GROUPS):
-            buf, zz, rows = self.part(g)
-            own = r["own_a"] if buf is r["attn"] else r["own_f"]
-
-            def sent(g=g, own=own, rows=rows, buf=buf):
-                dst = buf.at[self.z, self.c, self.slot, rows]
-                for k in range(3):
-                    remote(own.at[rows], dst, r["zs"].at[g, k], r["zr"].at[g, k], self.dev_z[k]).wait_send()
-
-            self.if_in(zz, sent)
-            for refs, s, v, t in (
-                (buf.at[zz, self.c, self.slot, rows], "as", "ar", self.dev_a),
-                (buf.at[zz, self.c, pl.ds(self.pair, 2), rows], "bs", "br", self.dev_b),
-                (buf.at[zz, self.c, :, rows], "cs", "cr", self.dev_c),
-            ):
-                remote(refs, refs, r[s].at[g], r[v].at[g], t).wait_send()
+        order = SCATTER[38]
+        ffn_left = max(i for i, s in enumerate(order) if s // 100 == 5 and s % 100 < W_OUT) + 1
+        relays_left = max(i for i, s in enumerate(order) if s // 100 < 5) + 1
+        for s in order[:ffn_left]:
+            self.one(s)
+        self.hand_over(FFN)
+        for s in order[ffn_left:relays_left]:
+            self.one(s)
+        self.take_vectors()
+        self.finish(FFN)
+        for s in order[relays_left:]:
+            self.one(s)
+        self.hand_over(ATT)
+        self.finish(ATT)
+        self.sent()
+
+    def head_copy(self, kind):
+        r, t = self.refs, self.g
+        count = (32, 48)[kind]
+        head, got = r[("flat_a", "flat_f")[kind]].at[pl.ds(0, count)], r["head_in"].at[pl.ds(32 * kind, count)]
+        return remote(head, got, r["hs"].at[2 * kind], r["hs"].at[2 * kind + 1], t.dev_before)
+
+    def hand_over(self, kind):
+        r, t = self.refs, self.g
+        total, flat = r[("attn_sum", "ffn_sum")[kind]], r[("flat_a", "flat_f")[kind]]
+        t.by_kind(kind, lambda tiles, n, at: t.from_tiles(total, flat, tiles, n, at))
+        pl.when(t.me > 0)(self.head_copy(kind).start)
+
+    def finish(self, kind):
+        r, t = self.refs, self.g
+        size, count, moved = ((ATT_ROWS, 32, 120), (FFN_ROWS, 48, 168))[kind]
+        flat, rows = r[("flat_a", "flat_f")[kind]], r[("rows_a", "rows_f")[kind]]
+        copy = self.head_copy(kind)
+        pl.when(t.me < 31)(copy.wait_recv)
+        mine = jnp.where(t.me == 31, r["vg"][32 * kind : 32 * kind + count, :], r["head_in"][32 * kind : 32 * kind + count, :])
+        flat[size : size + count, :] = mine
+        t.shifted(flat, rows, moved * t.me, size + 64)
+        whole = size * 128
+        out = r[("attn_out", "ffn_out")[kind]]
+        out[0:whole] = rows[0:size, :].reshape(whole)
+        if kind == ATT:
+            out[whole : whole + 120] = rows[size : size + 1, 0:120].reshape(120)
+        else:
+            out[whole : whole + 128] = rows[size : size + 1, :].reshape(128)
+            out[whole + 128 : whole + 168] = rows[size + 1 : size + 2, 0:40].reshape(40)
+        pl.when(t.me > 0)(copy.wait_send)
+
+
+class Kept:
+    def in_fc(self, m):
+        pass
+
+    in_in = between = pair_start = pair_end = tail = in_fc
 
 
 SCRATCH = dict(
+    x=((R, D), bf16),
+    mix=((R, D), bf16),
+    cot_b=((2, ROWS, D), bf16),
+    out_b=((2, ROWS, D), bf16),
     attn=((4, 2, 4, ATT_ROWS, 128), bf16),
     ffn=((4, 2, 4, FFN_ROWS, 128), bf16),
     vec=((VEC_ROWS, 128), f32),
     qx=((R, 1536), bf16),
     k=((R, D), bf16),
     v=((R, D), bf16),
-    mix=((R, D), bf16),
     xh1=((R, D), f32),
     rs1=((R, 128), f32),
     n1=((R, D), bf16),
@@ -664,64 +1167,87 @@
     gp=((R, FF), bf16),
     r2=((R, D), f32),
     gf=((R, D), bf16),
-    do=((R, D), bf16),
+    qkv_g=((3, 2, 4, ATT_ROWS, 128), bf16),
 )
 
 
-def run_layer(linked, length, x, cot, attn_in, ffn_in, vec_in):
+def run_layer(linked, length, x, cot, attn_in, ffn_in, vec_in=None):
     dma = pltpu.SemaphoreType.DMA
     vmem, anywhere = pl.BlockSpec(memory_space=pltpu.VMEM), pl.BlockSpec(memory_space=pl.ANY)
-    names = ["length", "x", "cot"] + (["own_a", "own_f", "own_v"] if linked else ["attn_in", "ffn_in", "vec_in"])
-    names += ["out", "gin", "attn_g", "ffn_g", "vg"]
-    scratch = [pltpu.VMEM(*s) for s in SCRATCH.values()]
-    names += list(SCRATCH)
+    names = ["length", "x_in", "cot"] + (["attn_own", "ffn_own"] if linked else ["attn_in", "ffn_in", "vec_in"])
+    names += ["out", "gin"] + (["attn_out", "ffn_out"] if linked else ["attn_g", "ffn_g", "vg"])
+    more = dict(io=dma((10,)))
     if linked:
-        sems = dict(
+        more.update(
+            vg=pltpu.VMEM((VEC_ROWS, 128), f32),
             vec_all=pltpu.VMEM((2, 4, VEC_ROWS, 128), bf16),
-            own_sem=dma((GROUPS,)),
-            zs=dma((GROUPS, 3)),
-            zr=dma((GROUPS, 3)),
-            vsem=dma((11,)),
-            **{k: dma((GROUPS,)) for k in ("as", "ar", "bs", "br", "cs", "cr")},
+            tail=pltpu.VMEM((VEC_ROWS, 128), bf16),
+            tail_in=pltpu.VMEM((VEC_ROWS, 128), bf16),
+            head_in=pltpu.VMEM((VEC_ROWS, 128), f32),
+            flat_a=pltpu.VMEM((704, 128), f32),
+            flat_f=pltpu.VMEM((1280, 128), f32),
+            rows_a=pltpu.VMEM((640, 128), f32),
+            rows_f=pltpu.VMEM((1216, 128), f32),
+            gs=dma((21,)),
+            zr=dma((N_GROUPS, 4)),
+            ar=dma((N_GROUPS, 4)),
+            br=dma((N_GROUPS, 4)),
+            cr=dma((N_GROUPS, 4)),
+            vsem=dma((13,)),
+            ss=dma((3, 6)),
+            sr=dma((4, N_ITEMS)),
+            vs=dma((6,)),
+            vr=dma((6,)),
+            hs=dma((4,)),
+            vg_r=pltpu.VMEM((6, VEC_ROWS, 128), f32),
         )
-    else:
-        sems = {}
-    sems["sems"] = dma((2,))
-    scratch += list(sems.values())
-    names += list(sems)
+        for kind, rows in (("attn", ATT_ROWS), ("ffn", FFN_ROWS)):
+            more[kind + "_rc"] = pltpu.VMEM((4, 4, rows, 128), bf16)
+            more[kind + "_rb"] = pltpu.VMEM((4, 2, rows, 128), bf16)
+            more[kind + "_ra"] = pltpu.VMEM((4, rows, 128), bf16)
+            more[kind + "_rz"] = pltpu.VMEM((3, rows, 128), bf16)
+            more[kind + "_sum"] = pltpu.VMEM((rows, 128), f32)
+    names += list(SCRATCH) + list(more)
+    scratch = [pltpu.VMEM(*s) for s in SCRATCH.values()] + list(more.values())
 
     def body(*args):
         refs = dict(zip(names, args, strict=True))
         refs["vg"][...] = jnp.zeros((VEC_ROWS, 128), f32)
-        layer_kernel((Gather if linked else Loaded)(refs), refs)
+        if linked:
+            gather = Gather(refs)
+            layer_kernel(gather, Scatter(refs, gather), refs)
+            return
+        layer_kernel(Loaded(refs), Kept(), refs)
         copies = [
-            pltpu.make_async_copy(refs["attn"], refs["attn_g"], refs["sems"].at[0]),
-            pltpu.make_async_copy(refs["ffn"], refs["ffn_g"], refs["sems"].at[1]),
+            pltpu.make_async_copy(refs["qkv_g"], refs["attn_g"].at[0:3], refs["io"].at[0]),
+            pltpu.make_async_copy(refs["attn"].at[3], refs["attn_g"].at[3], refs["io"].at[1]),
+            pltpu.make_async_copy(refs["ffn"], refs["ffn_g"], refs["io"].at[2]),
         ]
         for c in copies:
             c.start()
         for c in copies:
             c.wait()
 
-    big = anywhere if not linked else vmem
+    act_out = jax.ShapeDtypeStruct((R, D), bf16)
+    if linked:
+        grads = tuple(jax.ShapeDtypeStruct(a.shape, f32) for a in (attn_in, ffn_in))
+    else:
+        grads = tuple(jax.ShapeDtypeStruct(SCRATCH[k][0], bf16) for k in ("attn", "ffn"))
+        grads += (jax.ShapeDtypeStruct((VEC_ROWS, 128), f32),)
+    smem = pl.BlockSpec(memory_space=pltpu.SMEM)
+    args = (length, x, cot, attn_in, ffn_in) + (() if linked else (vec_in,))
     return pl.pallas_call(
         body,
-        out_shape=(
-            jax.ShapeDtypeStruct((R, D), bf16),
-            jax.ShapeDtypeStruct((R, D), bf16),
-            jax.ShapeDtypeStruct(SCRATCH["attn"][0], bf16),
-            jax.ShapeDtypeStruct(SCRATCH["ffn"][0], bf16),
-            jax.ShapeDtypeStruct((VEC_ROWS, 128), f32),
-        ),
-        in_specs=[pl.BlockSpec(memory_space=pltpu.SMEM), vmem, vmem, big, big, vmem],
-        out_specs=(vmem, vmem, anywhere, anywhere, vmem),
+        out_shape=(act_out, act_out) + grads,
+        in_specs=[smem, anywhere, anywhere] + ([vmem, vmem] if linked else [anywhere, anywhere, vmem]),
+        out_specs=(anywhere,) * 2 + ((vmem,) * 2 if linked else (anywhere, anywhere, vmem)),
         scratch_shapes=scratch,
         compiler_params=pltpu.CompilerParams(
             vmem_limit_bytes=64 * 1024 * 1024 - 65536,
             has_side_effects=True,
             **(dict(collective_id=0) if linked else {}),
         ),
-    )(length, x, cot, attn_in, ffn_in, vec_in)
+    )(*args)
 
 
 def qkv_chunk(flat):
@@ -752,35 +1278,7 @@
 
 
 def shards_linked(frames, lengths, attn_params, ffn_params, cotangent):
-    me = lax.axis_index("dp") * 4 + lax.axis_index("fsdp")
-    z = me // 8
-    tails = jnp.concatenate([attn_params[-ATT_VEC:], ffn_params[-FFN_VEC:]])
-    before = lax.ppermute(tails, AXES, [(i, i + 1) for i in range(31)])
-    a = lax.dynamic_slice(
-        jnp.concatenate([before[:ATT_VEC], attn_params]), (ATT_VEC - 120 * me,), (ATT_ROWS * 128,)
-    )
-    f = lax.dynamic_slice(
-        jnp.concatenate([before[ATT_VEC:], ffn_params]), (FFN_VEC - 168 * me,), (FFN_ROWS * 128,)
-    )
-    own_a = jnp.where(z == 3, tiled_chunk(a, 96, 6)[0], qkv_chunk(a)[0])
-    own_f = jnp.where(z >= 2, tiled_chunk(f, 192, 6)[0], tiled_chunk(f, 48, 24)[0])
-    own_v = pack_vectors(tails[:ATT_VEC], tails[ATT_VEC:])
-    out, gin, attn_g, ffn_g, vg = run_layer(True, lengths, frames[0], cotangent[0], own_a, own_f, own_v)
-
-    def scatter(g):
-        p0 = g[:, 0].reshape(4, 2, 2, -1, 128).transpose(0, 2, 1, 3, 4)
-        p1 = g[:, 1].reshape(4, 2, 2, -1, 128)
-        chunks = jnp.stack([p0, p1], axis=3).reshape(32, -1, 128)
-        return lax.psum_scatter(chunks.astype(f32), AXES, scatter_dimension=0, tiled=True)[0]
-
-    ga, gfn, vsum = scatter(attn_g), scatter(ffn_g), lax.psum(vg, AXES)
-    a = jnp.where(z == 3, tiled_flat(ga, 96, 6), qkv_flat(ga))
-    f = jnp.where(z >= 2, tiled_flat(gfn, 192, 6), tiled_flat(gfn, 48, 24))
-    heads = jnp.concatenate([a[:ATT_VEC], f[:FFN_VEC]])
-    vecs = jnp.concatenate([vsum[:30].reshape(-1), vsum[32:74].reshape(-1)])
-    after = jnp.where(me == 31, vecs, lax.ppermute(heads, AXES, [(i + 1, i) for i in range(31)]))
-    attn_grad = lax.dynamic_slice(jnp.concatenate([a, after[:ATT_VEC]]), (120 * me,), attn_params.shape)
-    ffn_grad = lax.dynamic_slice(jnp.concatenate([f, after[ATT_VEC:]]), (168 * me,), ffn_params.shape)
+    out, gin, attn_grad, ffn_grad = run_layer(True, lengths, frames[0], cotangent[0], attn_params, ffn_params)
     return out[None], gin[None], attn_grad, ffn_grad
 
 
@@ -811,10 +1309,10 @@
     vec_in = pack_vectors(attn_flat[ATT_MAT : ATT_MAT + ATT_VEC], ffn_flat[FFN_MAT : FFN_MAT + FFN_VEC])
     outs, gins, sums = [], [], None
     for u in range(frames.shape[0]):
-        out, gin, *grads = run_layer(False, lengths[u : u + 1], frames[u], cotangent[u], attn_in, ffn_in, vec_in)
+        out, gin, attn_g, ffn_g, vg = run_layer(False, lengths[u : u + 1], frames[u], cotangent[u], attn_in, ffn_in, vec_in)
         outs.append(out)
         gins.append(gin)
-        grads = [g.astype(f32) for g in grads]
+        grads = [g.astype(f32) for g in (attn_g, ffn_g, vg)]
         sums = grads if sums is None else [s + g for s, g in zip(sums, grads)]
     attn_c, ffn_c = from_places(sums[0]), from_places(sums[1])
     pad_a = attn_params.shape[0] * devices - ATT_MAT - ATT_VEC

time: 554 us -> 172 us (0.31)
  waiting for transfers between devices: 275 us -> 0 us
  blocking collectives: 43.2 us -> 0 us
  other arithmetic: 34.7 us -> 0 us
  local copies, waits for them, and re-layouts: 22.5 us -> 5.18 us
  between operations: 15 us -> 1.3 us
  Pallas kernels: 155 us -> 165 us
  starting transfers between devices: 8.39 us -> 0 us
    reduce_scatter x2 -> x0, waiting for transfers between devices: 272 us -> none  [scatter(): lax.psum_scatter(chunks.astype(f32), AXES, scatter_dimension=0, tiled=True)]
    psum x1 -> x0, blocking collectives: 43.2 us -> none  [shards_linked(): ga, gfn, vsum = (scatter(attn_g), scatter(ffn_g), lax.psum(vg, AXES))]
    convert_element_type x2 -> x0, other arithmetic: 18.7 us -> none  [scatter(): chunks.astype(f32)]
    pallas_call x1, Pallas kernels: 155 us -> 165 us  [run_layer(): pl.pallas_call(body, out_shape=(act_out, act_out) + grads, in_specs=[smem...]
    slice x8 -> x0, local copies, waits for them, and re-layouts: 9.72 us -> none  [the longest x2 9.69 us: scatter(): p0 = g[:, 0].reshape(4, 2, 2, -1, 128).transpose(0, 2, 1, 3, 4)]
    another operation x2 -> x0, other arithmetic: 9.18 us -> none  [scatter(): chunks = jnp.stack([p0, p1], axis=3).reshape(32, -1, 128)]
    ppermute x2 -> x0, starting transfers between devices: 8.31 us -> none  [the longest x1 4.54 us: shards_linked(): before = lax.ppermute(tails, AXES, [(i, i + 1) for i in range(31)])]
    another operation x6 -> x0, local copies, waits for them, and re-layouts: 7.81 us -> none  [the longest x3 3.97 us: tiled_flat(): return chunk.reshape(-1, tiles, rows, 128).transpose(0, 2, 1, 3).reshape(-1)]
  transfers between devices with their start and end apart: 4 -> 0, of which waited for: 3 -> 0; matrix products, arithmetic and copies ran while one was open for 6% -> 0% of each run, Pallas kernels for 0% -> 0%
where the time goes in v2:
time: 172 us
  Pallas kernels  165 us (96%)
  local copies, waits for them, and re-layouts  5.18 us (3%)
    pallas_call x1, Pallas kernels, run_layer(): pl.pallas_call(body, out_shape=(act_out, act_out) + grads, in_specs=[smem...  165 us
    unnamed x10, local copies, waits for them, and re-layouts  5.18 us

profile of v2, /device:TPU:1, one launch (start us, length us, event | category | flops | bytes accessed | tf_op | source)
XLA Modules:
  0.0 171.7 jit_solution(13420729171489956226)
XLA Ops:
  1.3 165.3 %shard_map.84 = (bf16[768,768]{1,0:T(8,128)(2,1)}, bf16[768,768]{1,0:T(8,128)(2,1)}, f32[73848]{0:T(1024)}, f32[147624]{0:T(1024)}) custom-call(s32[1]{0:T(128)S(6)} %copy.13.args_0_, bf16[768,768]{1,0:T(8,128)(2,1)} %bitcast.4, bf16[768,768]{1,0:T(8,128)(2,1)} %bitcast.5, bf16[73848]{0:T(1024)(128)(2,1)} %args_3_.4, bf16[147624]{0:T(1024)(128)(2,1)} %args_4_.4), custom_call_target="tpu_custom_call" | custom-call | tf_op jit(solution)/shard_map/pallas_call | solution.py:1239
  166.5 0.0 copy-start
  166.5 2.5 %copy.14 = bf16[1,768,768]{2,1,0:T(8,128)(2,1)} copy(bf16[1,768,768]{2,1,0:T(8,128)(2,1)} %bitcast.7) | data formatting | bytes 2359296
  169.0 0.0 copy-done
  169.0 0.0 copy-start.2
  169.0 0.0 copy-start.1
  169.0 1.0 copy.15
  170.0 0.1 copy-done.2
  170.1 0.7 copy.16
  170.9 0.0 copy-done.1
  170.9 0.9 copy.17
Async XLA Ops:
  166.5 2.5 %copy-start = (bf16[768,768]{1,0:T(8,128)(2,1)S(1)}, bf16[768,768]{1,0:T(8,128)(2,1)}, u32[]{:S(2)}) copy-start(bf16[768,768]{1,0:T(8,128)(2,1)} %get-tuple-element.9) | copy-start | bytes 3538948
  169.0 1.1 copy-start.2
  169.0 1.9 %copy-start.1 = (f32[147624]{0:T(1024)S(1)}, f32[147624]{0:T(1024)}, u32[]{:S(2)}) copy-start(f32[147624]{0:T(1024)} %get-tuple-element.19) | copy-start | bytes 1771492

commit v3 on v2

--- a/solution.py
+++ b/solution.py
@@ -145,11 +145,12 @@
     )
 
 
-def put_w_fc_rows(ffn, m, value):
+def put_w_fc_rows(ffn, m, value, tiles=range(6), base=0):
     z, at = chip_slot(m)
+    z = z - base
     for c in range(2):
-        for j in range(6):
-            ffn[z, c, at[c], 192 * j : 192 * j + 192, :] = value[192 * c : 192 * c + 192, 128 * j : 128 * j + 128]
+        for n, j in enumerate(tiles):
+            ffn[z, c, at[c], 192 * j : 192 * j + 192, :] = value[192 * c : 192 * c + 192, 128 * n : 128 * n + 128]
 
 
 def wide(vec, row, n=6):
@@ -352,7 +353,15 @@
     put_wide(vg, B2, d_b2)
     put_wide(vg, B_FC, d_bfc)
 
-    def back_fc(m, carry):
+    def back_first(m, carry):
+        scatter.in_first(m)
+        grad = tn(act[:, aligned(m * 384, 384)], gf[:, 0:384]).astype(bf16)
+        put_w_fc_rows(refs["fc_g"], m, grad, range(0, 3), 2)
+        return carry
+
+    lax.fori_loop(0, 4, back_first, 0)
+
+    def back_hidden(m):
         scatter.in_fc(m)
         cols = aligned(m * 384, 384)
         grad_act = nt(gf[...], w_fc_rows(ffn, m))
@@ -361,10 +370,20 @@
         sums = column_sum(low)
         for j in range(3):
             vg[pl.ds(B_IN + 3 * m + j, 1), :] = sums[:, 128 * j : 128 * j + 128]
+        return cols
+
+    def back_near(m, carry):
+        cols = back_hidden(m)
+        put_w_fc_rows(ffn, m, tn(act[:, cols], gf[:, 384:768]).astype(bf16), range(3, 6))
+        return carry
+
+    def back_fc(m, carry):
+        cols = back_hidden(m)
         put_w_fc_rows(ffn, m, tn(act[:, cols], gf[...]).astype(bf16))
         return carry
 
-    lax.fori_loop(0, 8, back_fc, 0)
+    lax.fori_loop(0, 4, back_near, 0)
+    lax.fori_loop(4, 8, back_fc, 0)
 
     def back_in(j, carry):
         scatter.in_in(j)
@@ -478,67 +497,73 @@
     )
 
 
-ATT_GROUPS = (192, 192, 192)
-FFN_GROUPS = (192, 96, 288, 288, 288)
+ATT_GROUPS = (288, 288)
+FFN_GROUPS = (192, 96, 192, 192, 192, 288)
 PLANE_GROUPS = 2
 Z, PASS, A, B, C, HOP = range(1, 7)
 VECTOR_MARKS = (3003, 4003, 5003)
 GATHER_ENDS = {
-    0: (3030, 3040, 1000, 1010, 1020, 1050, 3000, 3010, 3020, 3050, 3060, 3070, 4030, 4040, 3001, 4000, 4010, 4020, 3011, 4050, 3002, 3021, 6030, 6040, 1060, 1070, 4060, 4070, 3003, 5000, 3012, 4001, 4011, 5010, 4002, 3022, 4021, 5020, 4003, 6031, 4012, 4022, 5050, 6041, 3013, 5060, 3023, 5070, 3051, 4013, 5001, 4023, 3061, 5011, 4051, 5002, 3071, 3052, 4061, 5021, 3053, 5003,),
-    2: (5012, 4052, 4071, 3062,),
-    4: (6032, 5013, 5022, 4053, 5023,),
-    6: (6042, 5051, 4062, 3072, 3063,),
-    8: (5052, 5061, 3073,),
-    10: (4072,),
-    12: (5071, 4063, 4073,),
-    13: (5053, 5062,),
-    14: (6033, 5063, 6043, 5072,),
-    15: (5073,),
+    0: (3020, 3030, 1000, 1010, 1040, 3000, 3040, 3050, 3060, 3010, 3070, 4020, 4030, 4000, 3001, 4040, 3011, 6020, 4010, 6030, 1050, 1060, 1070, 3002, 3003, 4001, 5000, 4011, 5040, 4002, 3012, 4003, 6021, 5010, 6031, 4012, 5001, 3013, 5011, 3041, 5002, 3051, 4050, 4013, 3061, 3042, 5003,),
+    2: (4041, 3043, 3052, 4042, 4051, 3071, 5012, 5050,),
+    4: (4060, 3062, 5013,),
+    6: (5041, 4043, 6022, 4052,),
+    8: (5042, 5051, 4061, 6032, 4070, 3072, 5060,),
+    10: (5043, 5052, 3053, 3063, 4062,),
+    12: (5061, 4071, 3073,),
+    13: (5070, 5062, 4053, 4063, 4072,),
+    14: (6023, 5071, 4073,),
+    15: (5053, 6033, 5063,),
+    17: (5072,),
+    18: (5073,),
 }
 GATHER_MIDDLE = {
-    0: (3030, 3040, 1000, 1010, 1020, 3000, 3010, 3020, 3050, 3060, 3070, 4030, 4040, 3001, 3002, 4000, 4010, 4020, 2003, 3003, 3011, 4050, 6030, 3012, 6040, 4060, 2013, 3013, 3021, 4070, 5000, 3022, 4001, 4002, 5010, 2023, 1050, 1060, 1070, 4003, 3023, 4011, 5020, 3051, 4012, 4013, 4021, 2053, 5050, 3053, 4022, 6032, 4023, 5060, 6042, 6031, 4051, 3052, 4053, 6041, 5070, 5001, 3061, 5002, 4052, 5003, 3062, 4061, 2063, 3063,),
-    2: (5011, 5012, 3071,),
-    4: (5013, 2073, 4062, 4063, 5021, 3072, 3073,),
-    6: (5022, 4071,),
-    8: (5023, 4072, 4073, 5051,),
-    10: (6033, 5053,),
-    12: (6043, 5052, 5061,),
-    13: (5062, 5063,),
-    14: (5071,),
-    15: (5072,),
-    17: (5073,),
+    0: (3020, 3030, 1000, 1010, 3000, 3040, 3050, 3060, 3010, 3070, 4020, 4030, 4000, 4040, 3002, 2003, 3003, 6020, 3001, 4010, 6030, 3012, 4002, 2013, 1040, 1050, 1060, 1070, 5000, 4003, 3011, 3013, 5040, 4001, 2043, 3043, 3041, 4012, 5010, 4011, 6022, 4013, 6021, 5002, 6032, 3042, 6031, 5003, 5001, 2053, 3053, 3051, 3052,),
+    2: (4041, 5012,),
+    4: (2063, 4050, 3061, 4042, 4051, 3062, 3063, 5011, 5013,),
+    6: (2073, 5041, 4060, 3071, 3072, 3073,),
+    8: (5050, 5042, 4043, 4052,),
+    10: (5051, 4061,),
+    12: (6023, 5060, 4070, 5043, 4053,),
+    13: (6033, 5052, 5061, 4062, 4071,),
+    14: (5070, 5053, 4063, 4072,),
+    15: (5062, 4073,),
+    16: (5071,),
+    17: (5063,),
+    19: (5072, 5073,),
 }
 SCATTER = {
-    4: (100, 101, 102, 103,),
-    5: (200,),
-    6: (201, 202, 203,),
-    8: (300, 104, 105, 106, 107,),
-    9: (301, 204, 205, 108,),
-    10: (302, 206, 207, 400, 208, 109,),
-    11: (401, 303, 209, 110,),
-    12: (402, 210, 111,),
-    13: (304, 211, 403, 112,),
-    14: (305, 212, 113, 500,),
-    15: (404, 306, 213, 405, 307,),
-    16: (501,),
+    0: (100, 101,),
+    2: (200, 201,),
+    4: (102, 103,),
+    5: (202,),
+    6: (300, 203,),
+    7: (301,),
+    8: (302, 104, 105, 106, 107,),
+    9: (400, 204, 205, 206, 108,),
+    10: (401, 402, 303, 207, 208, 109,),
+    11: (304, 209, 110,),
+    12: (403, 210, 305, 111, 500,),
+    13: (211, 404, 112,),
+    14: (306, 212, 113,),
+    15: (501, 405, 307, 213, 406,),
+    16: (502, 308,),
     17: (114,),
-    19: (502, 406, 308, 407, 214,),
-    20: (503, 309, 115,),
-    22: (408, 310, 215, 504,),
-    23: (116,),
-    25: (409, 410, 311, 216, 505,),
-    26: (312, 117,),
-    28: (411, 313, 217,),
-    29: (506, 118,),
-    31: (508, 412, 413, 218, 314, 509,),
-    32: (507, 119,),
-    34: (315, 316, 219, 510,),
-    35: (414, 120,),
-    36: (317, 220,),
-    37: (511, 415, 318,),
-    38: (416, 512, 417, 319, 418, 320, 419, 513, 420, 514, 515, 516, 517, 518, 519, 520,),
+    19: (503, 309, 407, 214, 408,),
+    20: (310, 504, 115,),
+    22: (409, 311, 215,),
+    23: (116, 505,),
+    25: (410, 411, 312, 216,),
+    26: (506, 313, 117,),
+    28: (508, 509, 412, 217,),
+    29: (507, 118,),
+    31: (314, 413, 315, 510, 218,),
+    32: (316, 119,),
+    34: (414, 511, 317, 219,),
+    35: (415, 318, 120,),
+    36: (416, 220,),
+    37: (512, 417,),
+    38: (418, 319, 513, 320, 419, 515, 420, 514, 516, 517, 518, 519, 520,),
 }
-
 
 ATT, FFN = 0, 1
 
@@ -748,11 +773,17 @@
     def place_own(self, kind):
         r = self.refs
         if kind == ATT:
-            flat, rows, head, size, moved, at = r["flat_a"], r["rows_a"], ATT_HEAD, ATT_ROWS, 120, 0
+            flat, rows, head, size, moved, at = r["flat_a"], r["attn_sum"], ATT_HEAD, ATT_ROWS, 120, 0
         else:
-            flat, rows, head, size, moved, at = r["flat_f"], r["rows_f"], FFN_HEAD, FFN_ROWS, 168, 32
+            flat, rows, head, size, moved, at = r["flat_f"], r["ffn_sum"], FFN_HEAD, FFN_ROWS, 168, 32
         flat[0:head, :] = r["tail_in"][at : at + head, :].astype(f32)
-        self.shifted(flat, rows, head * 128 - moved * self.me, size)
+        shift = head * 128 - moved * self.me
+
+        def step(n, carry):
+            rows[pl.ds(pl.multiple_of(n * 64, 64), 64), :] = self.shifted(flat, shift, n)
+            return carry
+
+        lax.fori_loop(0, size // 64, step, 0)
         slot = self.buf[kind].at[self.z, self.c, self.slot]
         self.by_kind(kind, lambda tiles, n, at: self.to_tiles(rows, slot, tiles, n, at))
 
@@ -772,18 +803,13 @@
         for t in range(tiles):
             flat[pl.ds(t, n, stride=tiles), :] = total[at(t) : at(t) + n, :]
 
-    def shifted(self, src, dst, shift, count):
+    def shifted(self, src, shift, n):
         row, turn = lax.div(shift, 128), lax.rem(shift, 128)
-
-        def step(n, carry):
-            lane = lax.broadcasted_iota(jnp.int32, (64, 128), 1)
-            back = lax.rem(128 - turn, 128)
-            low = pltpu.roll(src[pl.ds(n * 64 + row, 64), :], back, 1)
-            high = pltpu.roll(src[pl.ds(n * 64 + row + 1, 64), :], back, 1)
-            dst[pl.ds(pl.multiple_of(n * 64, 64), 64), :] = jnp.where(lane < 128 - turn, low, high)
-            return carry
-
-        lax.fori_loop(0, count // 64, step, 0)
+        lane = lax.broadcasted_iota(jnp.int32, (64, 128), 1)
+        back = lax.rem(128 - turn, 128)
+        low = pltpu.roll(src[pl.ds(n * 64 + row, 64), :], back, 1)
+        high = pltpu.roll(src[pl.ds(n * 64 + row + 1, 64), :], back, 1)
+        return jnp.where(lane < 128 - turn, low, high)
 
     def start(self):
         self.load_own()
@@ -893,6 +919,8 @@
         self.refs, self.g = refs, gather
 
     def part(self, item):
+        if item < 2:
+            return "fc_g", "ffn", range(2, 3), pl.ds(288 * item, 288), 288, 0
         if item >= W_QKV:
             return "qkv_g", "attn", range(0, 3), pl.ds(96 * (item - W_QKV), 96), 96, 2
         if item == W_OUT:
@@ -905,6 +933,9 @@
     def span(self, zz):
         return pl.ds(zz[0], len(zz))
 
+    def at(self, buf, z):
+        return z - 2 if buf == "fc_g" else z
+
     def add(self, pairs, rows, count):
         def step(n, carry):
             at = pl.ds(pl.multiple_of(rows.start + n * 96, 96), 96)
@@ -922,7 +953,7 @@
         buf, kind, zz, rows, _, s = self.part(g)
         r, t = self.refs, self.g
         return remote(
-            r[buf].at[self.span(zz), 1 - t.c, :, rows],
+            r[buf].at[self.span([self.at(buf, z) for z in zz]), 1 - t.c, :, rows],
             r[kind + "_rc"].at[self.span(zz), :, rows],
             r["ss"].at[s, 0],
             r["sr"].at[0, g],
@@ -933,7 +964,7 @@
         buf, kind, zz, rows, _, s = self.part(g)
         r, t = self.refs, self.g
         return remote(
-            r[buf].at[self.span(zz), t.c, pl.ds(t.other_pair, 2), rows],
+            r[buf].at[self.span([self.at(buf, z) for z in zz]), t.c, pl.ds(t.other_pair, 2), rows],
             r[kind + "_rb"].at[self.span(zz), :, rows],
             r["ss"].at[s, 1],
             r["sr"].at[1, g],
@@ -944,7 +975,7 @@
         buf, kind, zz, rows, _, s = self.part(g)
         r, t = self.refs, self.g
         return remote(
-            r[buf].at[self.span(zz), t.c, t.other_slot, rows],
+            r[buf].at[self.span([self.at(buf, z) for z in zz]), t.c, t.other_slot, rows],
             r[kind + "_ra"].at[self.span(zz), rows],
             r["ss"].at[s, 2],
             r["sr"].at[2, g],
@@ -955,7 +986,7 @@
         buf, kind, zz, rows, _, s = self.part(g)
         r, t = self.refs, self.g
         return remote(
-            r[buf].at[t.zs[k], t.c, t.slot, rows],
+            r[buf].at[self.at(buf, t.zs[k]), t.c, t.slot, rows],
             r[kind + "_rz"].at[k, rows],
             r["ss"].at[s, 3 + k],
             r["sr"].at[3, g],
@@ -972,21 +1003,21 @@
         buf, kind, zz, rows, n, _ = self.part(g)
         r, t = self.refs, self.g
         self.c_copy(g).wait_recv()
-        self.add([(r[buf].at[z, t.c, i], r[kind + "_rc"].at[z, i]) for z in zz for i in range(4)], rows, n)
+        self.add([(r[buf].at[self.at(buf, z), t.c, i], r[kind + "_rc"].at[z, i]) for z in zz for i in range(4)], rows, n)
         self.b_copy(g).start()
 
     def a_send(self, g):
         buf, kind, zz, rows, n, _ = self.part(g)
         r, t = self.refs, self.g
         self.b_copy(g).wait_recv()
-        self.add([(r[buf].at[z, t.c, t.pair + i], r[kind + "_rb"].at[z, i]) for z in zz for i in range(2)], rows, n)
+        self.add([(r[buf].at[self.at(buf, z), t.c, t.pair + i], r[kind + "_rb"].at[z, i]) for z in zz for i in range(2)], rows, n)
         self.a_copy(g).start()
 
     def z_send(self, g):
         buf, kind, zz, rows, n, _ = self.part(g)
         r, t = self.refs, self.g
         self.a_copy(g).wait_recv()
-        self.add([(r[buf].at[z, t.c, t.slot], r[kind + "_ra"].at[z]) for z in zz], rows, n)
+        self.add([(r[buf].at[self.at(buf, z), t.c, t.slot], r[kind + "_ra"].at[z]) for z in zz], rows, n)
         for k in range(3):
 
             @pl.when(self.inside(t.zs[k], zz))
@@ -1004,7 +1035,7 @@
 
             def step(i, carry):
                 at = pl.ds(pl.multiple_of(rows.start + i * 96, 96), 96)
-                total = r[buf][t.z, t.c, t.slot, at, :].astype(f32)
+                total = r[buf][self.at(buf, t.z), t.c, t.slot, at, :].astype(f32)
                 for k in range(3):
                     total = total + r[kind + "_rz"][k, at, :].astype(f32)
                 r[kind + "_sum"][at, :] = total
@@ -1072,6 +1103,9 @@
         for v in range(count):
             if first + stride * v in SCATTER:
                 pl.when(i == v)(lambda v=v: self.step(first + stride * v))
+
+    def in_first(self, m):
+        self.loop(m, 40, 1, 4)
 
     def in_fc(self, m):
         self.loop(m, 0, 1, 8)
@@ -1125,20 +1159,24 @@
     def finish(self, kind):
         r, t = self.refs, self.g
         size, count, moved = ((ATT_ROWS, 32, 120), (FFN_ROWS, 48, 168))[kind]
-        flat, rows = r[("flat_a", "flat_f")[kind]], r[("rows_a", "rows_f")[kind]]
+        flat, out = r[("flat_a", "flat_f")[kind]], r[("attn_out", "ffn_out")[kind]]
         copy = self.head_copy(kind)
         pl.when(t.me < 31)(copy.wait_recv)
         mine = jnp.where(t.me == 31, r["vg"][32 * kind : 32 * kind + count, :], r["head_in"][32 * kind : 32 * kind + count, :])
         flat[size : size + count, :] = mine
-        t.shifted(flat, rows, moved * t.me, size + 64)
+
+        def step(n, carry):
+            out[pl.ds(pl.multiple_of(n * 8192, 8192), 8192)] = t.shifted(flat, moved * t.me, n).reshape(8192)
+            return carry
+
+        lax.fori_loop(0, size // 64, step, 0)
         whole = size * 128
-        out = r[("attn_out", "ffn_out")[kind]]
-        out[0:whole] = rows[0:size, :].reshape(whole)
+        rest = t.shifted(flat, moved * t.me, size // 64)
         if kind == ATT:
-            out[whole : whole + 120] = rows[size : size + 1, 0:120].reshape(120)
+            out[whole : whole + 120] = rest[0:1, 0:120].reshape(120)
         else:
-            out[whole : whole + 128] = rows[size : size + 1, :].reshape(128)
-            out[whole + 128 : whole + 168] = rows[size + 1 : size + 2, 0:40].reshape(40)
+            out[whole : whole + 128] = rest[0:1, :].reshape(128)
+            out[whole + 128 : whole + 168] = rest[1:2, 0:40].reshape(40)
         pl.when(t.me > 0)(copy.wait_send)
 
 
@@ -1146,7 +1184,7 @@
     def in_fc(self, m):
         pass
 
-    in_in = between = pair_start = pair_end = tail = in_fc
+    in_first = in_in = between = pair_start = pair_end = tail = in_fc
 
 
 SCRATCH = dict(
@@ -1168,6 +1206,7 @@
     r2=((R, D), f32),
     gf=((R, D), bf16),
     qkv_g=((3, 2, 4, ATT_ROWS, 128), bf16),
+    fc_g=((1, 2, 4, FFN_ROWS // 2, 128), bf16),
 )
 
 
@@ -1186,8 +1225,6 @@
             head_in=pltpu.VMEM((VEC_ROWS, 128), f32),
             flat_a=pltpu.VMEM((704, 128), f32),
             flat_f=pltpu.VMEM((1280, 128), f32),
-            rows_a=pltpu.VMEM((640, 128), f32),
-            rows_f=pltpu.VMEM((1216, 128), f32),
             gs=dma((21,)),
             zr=dma((N_GROUPS, 4)),
             ar=dma((N_GROUPS, 4)),
@@ -1221,7 +1258,10 @@
         copies = [
             pltpu.make_async_copy(refs["qkv_g"], refs["attn_g"].at[0:3], refs["io"].at[0]),
             pltpu.make_async_copy(refs["attn"].at[3], refs["attn_g"].at[3], refs["io"].at[1]),
-            pltpu.make_async_copy(refs["ffn"], refs["ffn_g"], refs["io"].at[2]),
+            pltpu.make_async_copy(refs["ffn"].at[0:2], refs["ffn_g"].at[0:2], refs["io"].at[2]),
+            pltpu.make_async_copy(refs["fc_g"], refs["ffn_g"].at[2:3, :, :, 0:576], refs["io"].at[3]),
+            pltpu.make_async_copy(refs["ffn"].at[2:3, :, :, 576:], refs["ffn_g"].at[2:3, :, :, 576:], refs["io"].at[4]),
+            pltpu.make_async_copy(refs["ffn"].at[3], refs["ffn_g"].at[3], refs["io"].at[5]),
         ]
         for c in copies:
             c.start()
@@ -1250,6 +1290,31 @@
     )(*args)
 
 
+def copy_results(*arrays):
+    n = len(arrays)
+
+    def body(*refs):
+        src, dst, held, sems = refs[:n], refs[n : 2 * n], refs[2 * n : 3 * n], refs[3 * n]
+        takes = [pltpu.make_async_copy(src[i], held[i], sems.at[i]) for i in range(n)]
+        gives = [pltpu.make_async_copy(held[i], dst[i], sems.at[n + i]) for i in range(n)]
+        for copy in takes:
+            copy.start()
+        for take, give in zip(takes, gives):
+            take.wait()
+            give.start()
+        for copy in gives:
+            copy.wait()
+
+    anywhere = pl.BlockSpec(memory_space=pl.ANY)
+    return pl.pallas_call(
+        body,
+        out_shape=tuple(jax.ShapeDtypeStruct(a.shape, a.dtype) for a in arrays),
+        in_specs=[anywhere] * n,
+        out_specs=(anywhere,) * n,
+        scratch_shapes=[pltpu.VMEM(a.shape, a.dtype) for a in arrays] + [pltpu.SemaphoreType.DMA((2 * n,))],
+    )(*arrays)
+
+
 def qkv_chunk(flat):
     return flat.reshape(-1, 32, 3, 6, 128).transpose(0, 3, 2, 1, 4).reshape(-1, ATT_ROWS, 128)
 
@@ -1278,7 +1343,9 @@
 
 
 def shards_linked(frames, lengths, attn_params, ffn_params, cotangent):
-    out, gin, attn_grad, ffn_grad = run_layer(True, lengths, frames[0], cotangent[0], attn_params, ffn_params)
+    out, gin, attn_grad, ffn_grad = copy_results(
+        *run_layer(True, lengths, frames[0], cotangent[0], attn_params, ffn_params)
+    )
     return out[None], gin[None], attn_grad, ffn_grad
 
 

time: 172 us -> 166 us (0.965)
  local copies, waits for them, and re-layouts: 5.18 us -> 0 us
    unnamed x10 -> x0, local copies, waits for them, and re-layouts: 5.18 us -> none
    pallas_call x1, Pallas kernels: 165 us -> 161 us  [run_layer(): pl.pallas_call(body, out_shape=(act_out, act_out) + grads, in_specs=[smem...]
    pallas_call x0 -> x1, Pallas kernels: none -> 3.03 us  [copy_results(): pl.pallas_call(body, out_shape=tuple((jax.ShapeDtypeStruct(a.shape, a.dty...]
where the time goes in v3:
time: 166 us
  Pallas kernels  164 us (99%)
    pallas_call x1, Pallas kernels, run_layer(): pl.pallas_call(body, out_shape=(act_out, act_out) + grads, in_specs=[smem...  161 us

profile of v3, /device:TPU:1, one launch (start us, length us, event | category | flops | bytes accessed | tf_op | source)
XLA Modules:
  0.0 165.9 jit_solution(5385541313861266199)
XLA Ops:
  1.3 161.5 %shard_map.84 = (bf16[768,768]{1,0:T(8,128)(2,1)}, bf16[768,768]{1,0:T(8,128)(2,1)}, f32[73848]{0:T(1024)}, f32[147624]{0:T(1024)}) custom-call(s32[1]{0:T(128)S(6)} %copy.9.args_0_, bf16[768,768]{1,0:T(8,128)(2,1)} %bitcast.4, bf16[768,768]{1,0:T(8,128)(2,1)} %bitcast.5, bf16[73848]{0:T(1024)(128)(2,1)} %args_3_.4, bf16[147624]{0:T(1024)(128)(2,1)} %args_4_.4), custom_call_target="tpu_custom_call" | custom-call | tf_op jit(solution)/shard_map/pallas_call | solution.py:1279
  162.7 3.0 %shard_map.85 = (bf16[768,768]{1,0:T(8,128)(2,1)}, bf16[768,768]{1,0:T(8,128)(2,1)}, f32[73848]{0:T(1024)}, f32[147624]{0:T(1024)}) custom-call(bf16[768,768]{1,0:T(8,128)(2,1)} %get-tuple-element.12.refs_0_, bf16[768,768]{1,0:T(8,128)(2,1)} %get-tuple-element.13.refs_1_, f32[73848]{0:T(1024)} %get-tuple-element.14.refs_2_, f32[147624]{0:T(1024)} %get-tuple-element.15.refs_3_), custom_call_target="tpu_custom_call" | custom-call | tf_op jit(solution)/shard_map/pallas_call | solution.py:1309

commit v4 on v3

--- a/solution.py
+++ b/solution.py
@@ -613,11 +613,12 @@
         self.dev_before = (lax.div(before, 4), lax.rem(before, 4))
         self.buf = (refs["attn"], refs["ffn"])
 
-    def barrier(self):
+    def barrier(self, own_work):
         bar = pltpu.get_barrier_semaphore()
         targets = [self.dev_a, self.dev_b, self.dev_c, self.dev_after, self.dev_before] + self.dev_z
         for t in targets:
             pl.semaphore_signal(bar, inc=1, device_id=t, device_id_type=MESH)
+        own_work()
         pl.semaphore_wait(bar, len(targets))
 
     def z_copy(self, g, k):
@@ -812,8 +813,7 @@
         return jnp.where(lane < 128 - turn, low, high)
 
     def start(self):
-        self.load_own()
-        self.barrier()
+        self.barrier(self.load_own)
         pl.when(self.me < 31)(lambda: self.tail_copy().start())
         self.vectors(0)
         pl.when(self.me > 0)(lambda: self.tail_copy().wait_recv())
@@ -1127,15 +1127,19 @@
             self.step(35 + n)
             self.vectors(n)
             return
-        self.vectors(3)
         order = SCATTER[38]
         ffn_left = max(i for i, s in enumerate(order) if s // 100 == 5 and s % 100 < W_OUT) + 1
         relays_left = max(i for i, s in enumerate(order) if s // 100 < 5) + 1
-        for s in order[:ffn_left]:
+        at = order.index(300 + N_ITEMS - 1) + 1
+        for n, s in enumerate(order[:ffn_left]):
             self.one(s)
+            if n + 1 == at:
+                self.vectors(3)
         self.hand_over(FFN)
-        for s in order[ffn_left:relays_left]:
+        for n, s in enumerate(order[ffn_left:relays_left]):
             self.one(s)
+            if n + 1 + ffn_left == at:
+                self.vectors(3)
         self.take_vectors()
         self.finish(FFN)
         for s in order[relays_left:]:
@@ -1292,11 +1296,22 @@
 
 def copy_results(*arrays):
     n = len(arrays)
+    parts = [(i, p) for p in range(3) for i in range(n) if arrays[i].ndim == 2] + [
+        (i, None) for i in range(n) if arrays[i].ndim == 1
+    ]
 
     def body(*refs):
         src, dst, held, sems = refs[:n], refs[n : 2 * n], refs[2 * n : 3 * n], refs[3 * n]
-        takes = [pltpu.make_async_copy(src[i], held[i], sems.at[i]) for i in range(n)]
-        gives = [pltpu.make_async_copy(held[i], dst[i], sems.at[n + i]) for i in range(n)]
+
+        def view(ref, p):
+            return ref if p is None else ref.at[pl.ds(256 * p, 256)]
+
+        takes = [
+            pltpu.make_async_copy(view(src[i], p), view(held[i], p), sems.at[0, j]) for j, (i, p) in enumerate(parts)
+        ]
+        gives = [
+            pltpu.make_async_copy(view(held[i], p), view(dst[i], p), sems.at[1, j]) for j, (i, p) in enumerate(parts)
+        ]
         for copy in takes:
             copy.start()
         for take, give in zip(takes, gives):
@@ -1311,7 +1326,7 @@
         out_shape=tuple(jax.ShapeDtypeStruct(a.shape, a.dtype) for a in arrays),
         in_specs=[anywhere] * n,
         out_specs=(anywhere,) * n,
-        scratch_shapes=[pltpu.VMEM(a.shape, a.dtype) for a in arrays] + [pltpu.SemaphoreType.DMA((2 * n,))],
+        scratch_shapes=[pltpu.VMEM(a.shape, a.dtype) for a in arrays] + [pltpu.SemaphoreType.DMA((2, len(parts)))],
     )(*arrays)
 
 

time: 166 us -> 165 us (level)
  no operation moved by 1% of the time
where the time goes in v4:
time: 165 us
  Pallas kernels  163 us (99%)
    pallas_call x1, Pallas kernels, run_layer(): pl.pallas_call(body, out_shape=(act_out, act_out) + grads, in_specs=[smem...  161 us

profile of v4, /device:TPU:1, one launch (start us, length us, event | category | flops | bytes accessed | tf_op | source)
XLA Modules:
  0.0 164.9 jit_solution(16290623494328248141)
XLA Ops:
  1.3 160.6 %shard_map.84 = (bf16[768,768]{1,0:T(8,128)(2,1)}, bf16[768,768]{1,0:T(8,128)(2,1)}, f32[73848]{0:T(1024)}, f32[147624]{0:T(1024)}) custom-call(s32[1]{0:T(128)S(6)} %copy.9.args_0_, bf16[768,768]{1,0:T(8,128)(2,1)} %bitcast.4, bf16[768,768]{1,0:T(8,128)(2,1)} %bitcast.5, bf16[73848]{0:T(1024)(128)(2,1)} %args_3_.4, bf16[147624]{0:T(1024)(128)(2,1)} %args_4_.4), custom_call_target="tpu_custom_call" | custom-call | tf_op jit(solution)/shard_map/pallas_call | solution.py:1283
  161.9 2.8 %shard_map.85 = (bf16[768,768]{1,0:T(8,128)(2,1)}, bf16[768,768]{1,0:T(8,128)(2,1)}, f32[73848]{0:T(1024)}, f32[147624]{0:T(1024)}) custom-call(bf16[768,768]{1,0:T(8,128)(2,1)} %get-tuple-element.12.refs_0_, bf16[768,768]{1,0:T(8,128)(2,1)} %get-tuple-element.13.refs_1_, f32[73848]{0:T(1024)} %get-tuple-element.14.refs_2_, f32[147624]{0:T(1024)} %get-tuple-element.15.refs_3_), custom_call_target="tpu_custom_call" | custom-call | tf_op jit(solution)/shard_map/pallas_call | solution.py:1324

commit v5 on v4

--- a/solution.py
+++ b/solution.py
@@ -820,12 +820,15 @@
         self.place_own(ATT)
         for g in range(len(ATT_GROUPS)):
             self.run(1000 * Z + 10 * g)
+        for g in range(len(ATT_GROUPS)):
+            self.run(1000 * A + 10 * g)
         self.place_own(FFN)
         for who, table in ((self.is_end, GATHER_ENDS), (self.is_middle, GATHER_MIDDLE)):
 
             @pl.when(who)
             def _(table=table):
-                first = [v for v in table[0] if v >= 1000 * Z + 10 * len(ATT_GROUPS)]
+                done = [1000 * kind + 10 * g for kind in (Z, A) for g in range(len(ATT_GROUPS))]
+                first = [v for v in table[0] if v not in done]
                 cuts = [0] + [first.index(v) + 1 for v in VECTOR_MARKS] + [len(first)]
                 for stage in range(4):
                     for s in first[cuts[stage] : cuts[stage + 1]]:
@@ -1140,11 +1143,11 @@
             self.one(s)
             if n + 1 + ffn_left == at:
                 self.vectors(3)
-        self.take_vectors()
-        self.finish(FFN)
         for s in order[relays_left:]:
             self.one(s)
         self.hand_over(ATT)
+        self.take_vectors()
+        self.finish(FFN)
         self.finish(ATT)
         self.sent()
 

time: 165 us -> 165 us (level)
  no operation moved by 1% of the time
where the time goes in v5:
time: 165 us
  Pallas kernels  163 us (99%)
    pallas_call x1, Pallas kernels, run_layer(): pl.pallas_call(body, out_shape=(act_out, act_out) + grads, in_specs=[smem...  160 us

profile of v5, /device:TPU:1, one launch (start us, length us, event | category | flops | bytes accessed | tf_op | source)
XLA Modules:
  0.0 164.7 jit_solution(4041491311737573343)
XLA Ops:
  1.3 160.4 %shard_map.84 = (bf16[768,768]{1,0:T(8,128)(2,1)}, bf16[768,768]{1,0:T(8,128)(2,1)}, f32[73848]{0:T(1024)}, f32[147624]{0:T(1024)}) custom-call(s32[1]{0:T(128)S(6)} %copy.9.args_0_, bf16[768,768]{1,0:T(8,128)(2,1)} %bitcast.4, bf16[768,768]{1,0:T(8,128)(2,1)} %bitcast.5, bf16[73848]{0:T(1024)(128)(2,1)} %args_3_.4, bf16[147624]{0:T(1024)(128)(2,1)} %args_4_.4), custom_call_target="tpu_custom_call" | custom-call | tf_op jit(solution)/shard_map/pallas_call | solution.py:1286
  161.7 2.8 %shard_map.85 = (bf16[768,768]{1,0:T(8,128)(2,1)}, bf16[768,768]{1,0:T(8,128)(2,1)}, f32[73848]{0:T(1024)}, f32[147624]{0:T(1024)}) custom-call(bf16[768,768]{1,0:T(8,128)(2,1)} %get-tuple-element.12.refs_0_, bf16[768,768]{1,0:T(8,128)(2,1)} %get-tuple-element.13.refs_1_, f32[73848]{0:T(1024)} %get-tuple-element.14.refs_2_, f32[147624]{0:T(1024)} %get-tuple-element.15.refs_3_), custom_call_target="tpu_custom_call" | custom-call | tf_op jit(solution)/shard_map/pallas_call | solution.py:1327
